TPU v7x, 32 devices: a whole 2x2x4 slice. The times are simulated.
32 devices in a mesh: dp: 16 (over z, y, x), mp: 2 (over core).
Axes of the slice: x: 2, y: 2, z: 4, core: 2. Of those that a mesh axis runs over, the one named last changes fastest.
Arguments:
- tokens: bfloat16 [32768, 768], P('dp'), may hold values from -6 to 6
- segments: int32 [32768], P('dp'), may hold values from 0 to 31, as said below
- lengths: int32 [32, 32], P('dp'), may hold values from 0 to 1024, as said below
- ln1_gain: bfloat16 [768], replicated, may hold values from 0.25 to 1.75
- ln1_bias: bfloat16 [768], replicated, may hold values from -4 to 4
- w_qkv: bfloat16 [768, 3, 768], P(None, None, 'mp'), may hold values from -0.21875 to 0.21875
- b_qv: bfloat16 [2, 768], P(None, 'mp'), may hold values from -4 to 4
- w_out: bfloat16 [768, 768], P('mp'), may hold values from -0.625 to 0.625
- out_bias: bfloat16 [768], replicated, may hold values from -4 to 4
- ln2_gain: bfloat16 [768], replicated, may hold values from 0.25 to 1.75
- ln2_bias: bfloat16 [768], replicated, may hold values from -4 to 4
- w_fc: bfloat16 [768, 3072], P(None, 'mp'), may hold values from -0.21875 to 0.21875
- b_fc: bfloat16 [3072], P('mp'), may hold values from -4 to 4
- w_proj: bfloat16 [3072, 768], P('mp'), may hold values from -0.109375 to 0.109375
- proj_bias: bfloat16 [768], replicated, may hold values from -4 to 4
- cotangent: bfloat16 [32768, 768], P('dp'), may hold values from -17 to 17
Outputs:
- block_out: bfloat16 [32768, 768], P('dp')
- input_grad: float32 [32768, 768], P('dp')
- grad_ln1_gain: float32 [768], replicated
- grad_ln1_bias: float32 [768], replicated
- grad_w_qkv: float32 [768, 3, 768], P(None, None, 'mp')
- grad_b_qv: float32 [2, 768], P(None, 'mp')
- grad_w_out: float32 [768, 768], P('mp')
- grad_out_bias: float32 [768], replicated
- grad_ln2_gain: float32 [768], replicated
- grad_ln2_bias: float32 [768], replicated
- grad_w_fc: float32 [768, 3072], P(None, 'mp')
- grad_b_fc: float32 [3072], P('mp')
- grad_w_proj: float32 [3072, 768], P('mp')
- grad_proj_bias: float32 [768], replicated
Inputs may be any that keep to these rules, and one draw needn't show every extreme that they name: `segments`: within each bin of 1024 rows the document numbers start at 0, never fall and rise by one at each new document; a bin holds 1 to 32 documents; some bin holds 32. lengths[b, s] is the number of rows of bin b whose document number is s, 0 for numbers that the bin does not use; some bin is one document of 1024 rows.
All inputs are finite; a program needn't handle non-finite values.
Results may differ from a plain program's by a relative error of at most 0.009.
Values sent between devices are 32-bit elements; how exact they have to be, the bound alone decides.
A program may use at most 192 MiB of HBM per device.

v0:
```python
import functools

import jax
import jax.numpy as jnp
from jax import lax
from jax.experimental import pallas as pl
from jax.experimental.pallas import tpu as pltpu
from jax.sharding import PartitionSpec as P

HEAD_DIM = 64
BIN = 1024
PAIR = 2 * HEAD_DIM
BLOCK = 256
CHUNK = 256
SLOTS = 4
SENDS = 4
LANDS = 5

epsilon = 1e-05
gelu_scale = 0.7978845608028654
gelu_cubic = 0.044715
score_scale = 0.125
masked_score = -1e30

MESH = pl.DeviceIdType.MESH
F32 = jnp.float32
BF16 = jnp.bfloat16
VMEM_LIMIT = 64_000_000


def dot_nn(left, right):
    return lax.dot_general(left, right, (((1,), (0,)), ((), ())), preferred_element_type=F32)


def dot_nt(left, right):
    return lax.dot_general(left, right, (((1,), (1,)), ((), ())), preferred_element_type=F32)


def dot_tn(left, right):
    return lax.dot_general(left, right, (((0,), (0,)), ((), ())), preferred_element_type=F32)


def norm_parts(values):
    center = values - jnp.mean(values, axis=-1, keepdims=True)
    inverse = lax.rsqrt(jnp.mean(center * center, axis=-1, keepdims=True) + epsilon)
    return center * inverse, inverse


def norm_back(upstream, normal, inverse, gain):
    scaled = upstream * gain
    centered = scaled - jnp.mean(scaled, axis=-1, keepdims=True)
    return inverse * (centered - normal * jnp.mean(scaled * normal, axis=-1, keepdims=True))


def gelu_pair(values):
    square = values * values
    tangent = jnp.tanh(gelu_scale * (values + gelu_cubic * square * values))
    half = 0.5 * (1.0 + tangent)
    slope = half + 0.5 * values * (1.0 - tangent * tangent) * (
        gelu_scale + 3.0 * gelu_cubic * gelu_scale * square
    )
    return values * half, slope


def column_to_row(column):
    rows = column.shape[0]
    return jnp.broadcast_to(column, (rows, 128)).T[0:1]


def head_mask(head, scale):
    lane = lax.broadcasted_iota(jnp.int32, (1, PAIR), 1)
    return jnp.where(lane // HEAD_DIM == head, scale, 0.0).astype(BF16)


def attend_pair(qkv_ref, start_ref, attn_ref, lse_ref):
    lane = lax.broadcasted_iota(jnp.int32, (1, PAIR), 1)
    for block in range(BIN // BLOCK):
        rows = slice(block * BLOCK, (block + 1) * BLOCK)
        seen = (block + 1) * BLOCK
        queries = qkv_ref[0, 0, rows]
        key_rows = qkv_ref[0, 1, 0:seen]
        value_rows = qkv_ref[0, 2, 0:seen]
        j = lax.broadcasted_iota(jnp.int32, (BLOCK, seen), 1)
        i = lax.broadcasted_iota(jnp.int32, (BLOCK, seen), 0) + block * BLOCK
        visible = (j >= start_ref[rows]) & (j <= i)
        mixed = []
        for head in range(2):
            scores = dot_nt(queries * head_mask(head, score_scale), key_rows)
            scores = jnp.where(visible, scores, masked_score)
            highest = jnp.max(scores, axis=-1, keepdims=True)
            weights = jnp.exp(scores - highest)
            totals = jnp.sum(weights, axis=-1, keepdims=True)
            mixed.append(dot_nn(weights.astype(BF16), value_rows) / totals)
            lse_ref[0, head : head + 1, rows] = column_to_row(highest + jnp.log(totals))
        attn_ref[0, rows] = jnp.where(lane < HEAD_DIM, mixed[0], mixed[1]).astype(BF16)


def project_and_attend(h1, w_ref, bias_ref, start_ref, qkv_ref, attn_ref, lse_ref):
    for c in range(3):
        out = dot_nn(h1, w_ref[c].astype(BF16)) + bias_ref[c : c + 1]
        qkv_ref[0, c] = out.astype(BF16)
    attend_pair(qkv_ref, start_ref, attn_ref, lse_ref)


def own_front_kernel(
    mp_ref, x_ref, seg_ref, len_ref, gain_ref, shift_ref, w_ref, bias_ref,
    qkv_ref, attn_ref, lse_ref, h1_ref, start_ref, row_ref,
):
    @pl.when(pl.program_id(0) == 0)
    def _():
        gain = gain_ref[...].astype(F32)
        shift = shift_ref[...].astype(F32)
        for block in range(BIN // BLOCK):
            rows = slice(block * BLOCK, (block + 1) * BLOCK)
            normal, _ = norm_parts(x_ref[rows].astype(F32))
            h1_ref[rows] = (normal * gain + shift).astype(BF16)
        mine = mp_ref[0]
        count = len_ref.shape[1]
        seg = seg_ref[pl.ds(mine, 1), :].astype(F32)
        seg = jnp.broadcast_to(seg, (128, BIN)).T
        seg = seg[:, :count]
        label = lax.broadcasted_iota(jnp.int32, (BIN, count), 1).astype(F32)
        sizes = len_ref[pl.ds(mine, 1), :].astype(F32)
        start = jnp.sum(jnp.where(label < seg, sizes, 0.0), axis=1, keepdims=True)
        rows_of = jnp.sum(jnp.where(label == seg, 1.0, 0.0), axis=0, keepdims=True)
        first = jnp.sum(jnp.where(label < seg, rows_of, 0.0), axis=1, keepdims=True)
        start = jnp.maximum(start, first)
        start_ref[...] = start.astype(jnp.int32)
        row_ref[...] = column_to_row(start).astype(jnp.int32)

    project_and_attend(h1_ref[...], w_ref, bias_ref, start_ref, qkv_ref, attn_ref, lse_ref)


def other_front_kernel(h1_ref, start_ref, w_ref, bias_ref, qkv_ref, attn_ref, lse_ref):
    project_and_attend(h1_ref[...], w_ref, bias_ref, start_ref, qkv_ref, attn_ref, lse_ref)


def fixed(shape):
    return pl.BlockSpec(shape, lambda *_: (0,) * len(shape), pipeline_mode=pl.Buffered(1))


def front(mine, x, seg, lens, gain, shift, w_own, bias_own, width):
    model = x.shape[1]
    pairs = width // PAIR
    per_pair = [
        pl.BlockSpec((3, model, PAIR), lambda p, *_: (0, 0, p)),
        pl.BlockSpec((3, PAIR), lambda p, *_: (0, p)),
    ]
    outs = [
        pl.BlockSpec((1, 3, BIN, PAIR), lambda p, *_: (p, 0, 0, 0)),
        pl.BlockSpec((1, BIN, PAIR), lambda p, *_: (p, 0, 0)),
        pl.BlockSpec((1, 8, BIN), lambda p, *_: (p, 0, 0)),
    ]
    out_shapes = [
        jax.ShapeDtypeStruct((pairs, 3, BIN, PAIR), BF16),
        jax.ShapeDtypeStruct((pairs, BIN, PAIR), BF16),
        jax.ShapeDtypeStruct((pairs, 8, BIN), F32),
    ]
    cost = pl.CostEstimate(flops=6_000_000_000, bytes_accessed=10_000_000, transcendentals=0)
    params = pltpu.CompilerParams(vmem_limit_bytes=VMEM_LIMIT)
    own = pl.pallas_call(
        own_front_kernel,
        out_shape=out_shapes
        + [
            jax.ShapeDtypeStruct((BIN, model), BF16),
            jax.ShapeDtypeStruct((BIN, 1), jnp.int32),
            jax.ShapeDtypeStruct((1, BIN), jnp.int32),
        ],
        grid_spec=pltpu.PrefetchScalarGridSpec(
            num_scalar_prefetch=1,
            grid=(pairs,),
            in_specs=[
                pl.BlockSpec((BIN, model), lambda p, m: (m[0], 0)),
                fixed(seg.shape), fixed(lens.shape), fixed((1, model)), fixed((1, model)),
            ]
            + per_pair,
            out_specs=outs
            + [
                pl.BlockSpec((BIN, model), lambda p, *_: (0, 0)),
                pl.BlockSpec((BIN, 1), lambda p, *_: (0, 0)),
                pl.BlockSpec((1, BIN), lambda p, *_: (0, 0)),
            ],
        ),
        compiler_params=params,
        cost_estimate=cost,
        name="own_front",
    )

    def other(h1, start, w_other, bias_other):
        return pl.pallas_call(
            other_front_kernel,
            out_shape=out_shapes,
            grid=(pairs,),
            in_specs=[fixed((BIN, model)), fixed((BIN, 1))] + per_pair,
            out_specs=outs,
            compiler_params=params,
            cost_estimate=cost,
            name="other_front",
        )(h1, start, w_other, bias_other)

    return own(mine, x, seg, lens, gain, shift, w_own, bias_own), other


def halving_plan(order, rows):
    first, back = [], []
    size = rows
    for n, bit in enumerate(order):
        if n < len(order) - 1 and size % 16 == 0:
            size //= 2
            first.append((bit, size, 0))
            back.append((bit, size, 2))
        else:
            first.append((bit, size, 1))
    return first + back[::-1]


def color_orders(bits, odd):
    plain = list(range(bits))
    orders = [plain, plain, plain]
    if bits > 1:
        orders[1] = [1, 0] + plain[2:]
    if bits > 2:
        orders[2] = [2, 1, 0] + plain[3:] if odd else [2, 0, 1] + plain[3:]
    return orders


def color_plans(bits, odd):
    return [halving_plan(order, CHUNK) for order in color_orders(bits, odd)]


def attend_back_pair(half, place, qkv, dattn, lse_ref, row_ref, dk, dv, vec, pairs):
    dk[...] = jnp.zeros_like(dk)
    dv[...] = jnp.zeros_like(dv)
    pair = half * pairs + place
    dq_sum = jnp.zeros((1, PAIR), F32)
    for block in range(BIN // BLOCK):
        rows = slice(block * BLOCK, (block + 1) * BLOCK)
        seen = (block + 1) * BLOCK
        queries = qkv[pair, 0, rows]
        upstream = dattn[pair, rows]
        key_rows = qkv[pair, 1, 0:seen]
        value_rows = qkv[pair, 2, 0:seen]
        j = lax.broadcasted_iota(jnp.int32, (seen, BLOCK), 0)
        i = lax.broadcasted_iota(jnp.int32, (seen, BLOCK), 1) + block * BLOCK
        visible = (j >= row_ref[0:1, rows]) & (j <= i)
        dq = jnp.zeros((BLOCK, PAIR), F32)
        for head in range(2):
            masked_q = queries * head_mask(head, score_scale)
            masked_up = upstream * head_mask(head, 1.0)
            scores = dot_nt(key_rows, masked_q)
            probs = jnp.exp(scores - lse_ref[pair, head : head + 1, rows])
            probs = jnp.where(visible, probs, 0.0)
            dprobs = dot_nt(value_rows, masked_up)
            inner = jnp.sum(probs * dprobs, axis=0, keepdims=True)
            dscores = (probs * (dprobs - inner)).astype(BF16)
            dv[0:seen] = dv[0:seen] + dot_nn(probs.astype(BF16), masked_up)
            dk[0:seen] = dk[0:seen] + dot_nn(dscores, masked_q)
            dq = dq + dot_tn(dscores, key_rows * head_mask(head, 1.0))
        dq = (dq * score_scale).astype(BF16)
        qkv[pair, 0, rows] = dq
        dq_sum = dq_sum + jnp.sum(dq.astype(F32), axis=0, keepdims=True)
    dv_low = dv[...].astype(BF16)
    qkv[pair, 1] = dk[...].astype(BF16)
    qkv[pair, 2] = dv_low
    dv_sum = jnp.sum(dv_low.astype(F32), axis=0, keepdims=True)
    width = pairs * PAIR
    vec[half, 8:9, pl.ds(pl.multiple_of(place * PAIR, PAIR), PAIR)] = dq_sum
    vec[half, 8:9, pl.ds(pl.multiple_of(width + place * PAIR, PAIR), PAIR)] = dv_sum


def back_kernel(
    bits, groups,
    qkv_own_ref, qkv_other_ref, attn_own_ref, attn_other_ref, h1_ref, w3_own_ref, w3_other_ref,
    x_ref, cot_ref, wo_own_ref, wo_other_ref, wf_own_ref, wf_other_ref, wp_own_ref, wp_other_ref,
    lse_own_ref, lse_other_ref, row_ref, gain_ref, vec_in_ref, bfc_ref,
    op_ref, of_ref, oa_ref, oq_ref, ig_ref, sum_ref, vo_ref,
    acc, mpbuf, rbufs, qkv, dattn, attn, cot, x, tall, flip, total, dwide, first,
    wf, wp, wo, w3, act, slope, lse, dk, dv, vec, vrecv,
    ssem, rsem, mps, mpr, wsem, lsem, bsem, hsem, igsem, vsem,
):
    dp = lax.axis_index("dp")
    mp = lax.axis_index("mp")
    chunks = 3 * groups
    own_bits = [(dp // (1 << b)) % 2 for b in range(bits)]
    partner = [dp + (1 - 2 * own_bits[b]) * (1 << b) for b in range(bits)]
    plans = [color_plans(bits, odd) for odd in range(2)]
    stages = len(plans[0][0])
    flights = [2] + [1] * (stages - 2) + [2]
    offsets = [sum(flights[:s]) for s in range(stages + 1)]
    pairs = qkv_own_ref.shape[0]
    model = x_ref.shape[1]
    width = pairs * PAIR
    pieces = model // CHUNK

    my_rows = pl.ds(pl.multiple_of(mp * BIN, BIN), BIN)
    loads = []

    def load(src, dst):
        loads.append(pltpu.make_async_copy(src, dst, lsem.at[len(loads)]))

    load(attn_own_ref, attn.at[0:pairs])
    load(attn_other_ref, attn.at[pairs : 2 * pairs])
    load(wo_own_ref, wo.at[0])
    load(wo_other_ref, wo.at[1])
    load(x_ref.at[my_rows], x)
    load(cot_ref.at[my_rows], cot)
    early = len(loads)
    load(qkv_own_ref, qkv.at[0:pairs])
    load(qkv_other_ref, qkv.at[pairs : 2 * pairs])
    load(lse_own_ref, lse.at[0:pairs])
    load(lse_other_ref, lse.at[pairs : 2 * pairs])

    def block_loads(u, begin):
        slot = u % 2
        at = pl.ds(pl.multiple_of((u // 2) * CHUNK, CHUNK), CHUNK)
        for half, fc_ref, proj_ref in ((0, wf_own_ref, wp_own_ref), (1, wf_other_ref, wp_other_ref)):
            @pl.when(slot == half)
            def _():
                for item in (
                    pltpu.make_async_copy(fc_ref.at[:, at], wf.at[half], bsem.at[half, 0]),
                    pltpu.make_async_copy(proj_ref.at[at], wp.at[half], bsem.at[half, 1]),
                ):
                    item.start() if begin else item.wait()

    def w3_loads(q, begin):
        slot = q % 2
        at = pl.ds(pl.multiple_of((q // 2) * PAIR, PAIR), PAIR)
        for half, ref in ((0, w3_own_ref), (1, w3_other_ref)):
            @pl.when(slot == half)
            def _():
                for c in range(3):
                    item = pltpu.make_async_copy(ref.at[c, :, at], w3.at[half, c], hsem.at[half, c])
                    item.start() if begin else item.wait()

    def h1_load():
        return pltpu.make_async_copy(h1_ref, tall, lsem.at[9])

    for item in loads:
        item.start()
    block_loads(jnp.int32(0), True)

    barrier = pltpu.get_barrier_semaphore()
    for b in range(bits):
        pl.semaphore_signal(barrier, inc=1, device_id=(partner[b], mp), device_id_type=MESH)
    pl.semaphore_signal(barrier, inc=1, device_id=(dp, 1 - mp), device_id_type=MESH)
    pl.semaphore_wait(barrier, bits + 1)

    def walk(plan):
        base, found = 0, []
        for bit, size, kind in plan:
            found.append(base)
            if kind == 0:
                base = base + own_bits[bit] * size
            if kind == 2:
                base = base - own_bits[bit] * size
        return found

    starts = [[walk(plan) for plan in plans[odd]] for odd in range(2)]

    def place(c, color, s):
        sides = []
        for odd in range(2):
            bit, size, kind = plans[odd][color][s]
            sides.append((starts[odd][color][s], own_bits[bit], partner[bit]))
        if plans[0][color] == plans[1][color]:
            return sides[0]
        return [jnp.where(c % 2 == 0, even, odd) for even, odd in zip(*sides)]

    def lanes(color):
        share = model // 3
        return slice(color * share, (color + 1) * share)

    def copy(c, color, s):
        _, size, kind = plans[0][color][s]
        slot = c % SLOTS
        base, side, device = place(c, color, s)
        if kind == 0:
            base = base + (1 - side) * size
        src = acc.at[c, pl.ds(pl.multiple_of(base, 8), size), lanes(color)]
        dst = src if kind == 2 else rbufs[color][s].at[slot]
        return pltpu.make_async_remote_copy(
            src, dst, ssem.at[slot, color, s], rsem.at[slot, color, s],
            device_id=(device, mp), device_id_type=MESH,
        )

    def finish(c, color, s):
        _, size, kind = plans[0][color][s]
        copy(c, color, s).wait()
        if kind == 2:
            return
        base, side, _ = place(c, color, s)
        if kind == 0:
            base = base + side * size
        rows = pl.ds(pl.multiple_of(base, 8), size)
        acc[c, rows, lanes(color)] = acc[c, rows, lanes(color)] + rbufs[color][s][c % SLOTS]

    def mp_copy(c):
        slot, land = c % SENDS, c % LANDS
        return pltpu.make_async_remote_copy(
            acc.at[chunks + slot], mpbuf.at[land], mps.at[land], mpr.at[land],
            device_id=(dp, 1 - mp), device_id_type=MESH,
        )

    def mp_finish(c):
        mp_copy(c).wait()
        acc[c] = acc[c] + mpbuf[c % LANDS]

    def chunk_rows(n):
        return pl.ds(pl.multiple_of(n * CHUNK, CHUNK), CHUNK)

    def whole_copy(dst, c):
        return pltpu.make_async_copy(acc.at[c], dst, wsem.at[c % SLOTS, 0])

    def piece_copies(c):
        at = chunk_rows(c // 2)
        return [
            pltpu.make_async_copy(
                acc.at[c, :, n * CHUNK : (n + 1) * CHUNK],
                of_ref.at[n * CHUNK : (n + 1) * CHUNK, at],
                wsem.at[c % SLOTS, n],
            )
            for n in range(pieces)
        ]

    def write(c, begin):
        @pl.when((c < 2 * groups) & (c % 2 == 0))
        def _():
            item = whole_copy(op_ref.at[chunk_rows(c // 2)], c)
            item.start() if begin else item.wait()

        @pl.when((c < 2 * groups) & (c % 2 == 1))
        def _():
            for item in piece_copies(c):
                item.start() if begin else item.wait()

        for part in range(2):
            piece = 2 * (c - 2 * groups) + part
            rows = slice(part * PAIR, (part + 1) * PAIR)

            @pl.when((c >= 2 * groups) & (piece < pairs))
            def _():
                at = pl.ds(pl.multiple_of(piece * PAIR, PAIR), PAIR)
                item = pltpu.make_async_copy(acc.at[c, rows], oa_ref.at[at], wsem.at[c % SLOTS, 6 * part])
                item.start() if begin else item.wait()

            @pl.when((c >= 2 * groups) & (piece >= pairs))
            def _():
                across = pl.ds(pl.multiple_of((piece // pairs - 1) * PAIR, PAIR), PAIR)
                for n in range(6):
                    down = pl.ds(pl.multiple_of((n // 3) * width + (piece % pairs) * PAIR, PAIR), PAIR)
                    item = pltpu.make_async_copy(
                        acc.at[c, rows, n * PAIR : (n + 1) * PAIR],
                        oq_ref.at[n % 3, down, across],
                        wsem.at[c % SLOTS, 6 * part + n],
                    )
                    item.start() if begin else item.wait()

    middle_tick = 2 * groups
    attend_tick = middle_tick + 1
    input_tick = attend_tick + 2 * pairs
    late = chunks - 4
    late_tick = late + 4
    arrivals = [(middle_tick + 2, [0]), (middle_tick + 4, [1, 2]), (middle_tick + 6, [3]), (middle_tick + 8, [4, 5])]
    ticks = chunks + 4 + offsets[stages] + 1

    def at_stage(t, shift):
        since = t - shift
        early = (since >= 3) & (since < late + 3)
        last = (since >= late_tick) & (since < chunks + 4)
        c = jnp.where(since < late_tick, since - 3, since - late_tick + late)
        return jnp.clip(c, 0, chunks - 1), early | last

    def ring_tick(t):
        @pl.when((t >= 3) & (t % 2 == 1) & (t < middle_tick + 3))
        def _():
            mp_finish(t - 3)
            mp_finish(t - 2)

        for at, made in arrivals:
            @pl.when(t == at)
            def _():
                for n in made:
                    mp_finish(2 * groups + n)

        for s in range(stages):
            c, valid = at_stage(t, offsets[s + 1])

            @pl.when(valid)
            def _():
                for color in range(3):
                    finish(c, color, s)

        for s in list(range(stages)) + [-1]:
            c, valid = at_stage(t, offsets[s + 1])

            @pl.when(valid)
            def _():
                if s + 1 == stages:
                    write(c, True)
                else:
                    for color in range(3):
                        copy(c, color, s + 1).start()

    def begin_layer():
        for item in loads[:early]:
            item.wait()
        out_bias = vec_in_ref[0:1]
        gain = vec_in_ref[1:2]
        shift = vec_in_ref[2:3]
        vec[...] = jnp.zeros_like(vec)

        def step(block, carry):
            rows = pl.ds(pl.multiple_of(block * BLOCK, BLOCK), BLOCK)
            branch = out_bias
            for half in range(2):
                mixed = [attn[half * pairs + p, rows] for p in range(pairs)]
                branch = branch + dot_nn(jnp.concatenate(mixed, axis=1), wo[half].astype(BF16))
            r1 = x[rows].astype(F32) + branch
            first[rows] = r1
            total[rows] = r1
            dwide[rows] = jnp.zeros((BLOCK, model), F32)
            normal, _ = norm_parts(r1)
            h2 = (normal * gain + shift).astype(BF16)
            tall[rows] = h2
            flip[:, rows] = h2.T
            return carry

        lax.fori_loop(0, BIN // BLOCK, step, 0)

    def hidden_half(u):
        b, half = u // 2, u % 2
        block_loads(u, False)

        @pl.when(u + 1 < 2 * groups)
        def _():
            block_loads(u + 1, True)

        span = 2 * BLOCK
        wf_low = wf[half].astype(BF16)
        wp_low = wp[half].astype(BF16)
        bias = bfc_ref[pl.ds(half * groups + b, 1), :]
        df_sum = jnp.zeros((1, CHUNK), F32)
        for block in range(BIN // span):
            rows = slice(block * span, (block + 1) * span)
            pre = dot_nn(tall[rows], wf_low) + bias
            hidden, rise = gelu_pair(pre)
            hidden = hidden.astype(BF16)
            act[rows] = hidden
            total[rows] = total[rows] + dot_nn(hidden, wp_low)
            df = (dot_nt(cot[rows], wp_low) * rise).astype(BF16)
            slope[rows] = df
            df_sum = df_sum + jnp.sum(df.astype(F32), axis=0, keepdims=True)
            dwide[rows] = dwide[rows] + dot_nt(df, wf_low)

        vec[half, pl.ds(6 + b // pieces, 1), pl.ds(pl.multiple_of((b % pieces) * CHUNK, CHUNK), CHUNK)] = df_sum
        at = jnp.where(half == 0, 2 * b, chunks + (2 * b) % SENDS)
        acc[at] = dot_tn(act[...], cot[...])
        fc = dot_nn(flip[...], slope[...])
        for n in range(pieces):
            acc[at + 1, :, n * CHUNK : (n + 1) * CHUNK] = fc[n * CHUNK : (n + 1) * CHUNK]

        @pl.when(half == 1)
        def _():
            mp_copy(2 * b).start()
            mp_copy(2 * b + 1).start()

    def put_piece(half, piece, part, value):
        n = piece // 2
        at = jnp.where(half == 0, 2 * groups + n, chunks + (2 * groups + n) % SENDS)
        rows = pl.ds(pl.multiple_of((piece % 2) * PAIR, PAIR), PAIR)
        acc[at, rows, part * width : part * width + value.shape[1]] = value

    def sum_copies():
        local = pltpu.make_async_copy(total, sum_ref.at[my_rows], igsem.at[3])
        remote = pltpu.make_async_remote_copy(
            total, sum_ref.at[my_rows], igsem.at[4], igsem.at[5],
            device_id=(dp, 1 - mp), device_id_type=MESH,
        )
        return local, remote

    def middle_back():
        for item in sum_copies():
            item.start()
        gain = vec_in_ref[1:2]
        w3_loads(jnp.int32(0), True)

        def step(block, sums):
            rows = pl.ds(pl.multiple_of(block * BLOCK, BLOCK), BLOCK)
            normal, inverse = norm_parts(first[rows])
            up = dwide[rows]
            upstream = cot[rows].astype(F32)
            dr1 = upstream + norm_back(up, normal, inverse, gain)
            first[rows] = dr1
            dwide[rows] = jnp.zeros((BLOCK, model), F32)
            da = dr1.astype(BF16)
            tall[rows] = da
            for half in range(2):
                back = dot_nt(da, wo[half].astype(BF16)).astype(BF16)
                for p in range(pairs):
                    dattn[half * pairs + p, rows] = back[:, p * PAIR : (p + 1) * PAIR]
            return tuple(
                total_row + jnp.sum(item, axis=0, keepdims=True)
                for total_row, item in zip(sums, (da.astype(F32), up * normal, up, upstream))
            )

        sums = lax.fori_loop(0, BIN // BLOCK, step, (jnp.zeros((1, model), F32),) * 4)
        for half in range(2):
            for n in range(4):
                vec[half, 2 + n : 3 + n] = sums[n]
            mixed = jnp.concatenate([attn[half * pairs + p] for p in range(pairs)], axis=1)
            grad = dot_tn(mixed, tall[...])
            for piece in range(pairs):
                put_piece(half, piece, 0, grad[piece * PAIR : (piece + 1) * PAIR])
        mp_copy(2 * groups).start()
        h1_load().start()
        for item in loads[early:]:
            item.wait()

    def attend_half(q):
        p, half = q // 2, q % 2

        @pl.when(q + 1 < 2 * pairs)
        def _():
            w3_loads(q + 1, True)

        @pl.when(q == 0)
        def _():
            h1_load().wait()
            flip[...] = tall[...].T

        attend_back_pair(half, p, qkv, dattn, lse, row_ref, dk, dv, vec, pairs)
        w3_loads(q, False)
        pair = half * pairs + p
        low = jnp.concatenate([qkv[pair, c] for c in range(3)], axis=1)
        grad = dot_nn(flip[...], low)
        for n in range(2 * pairs):
            put_piece(half, pairs * (p + 1) + n % pairs, n // pairs, grad[n * PAIR : (n + 1) * PAIR])
        weights = jnp.concatenate([w3[half, c].astype(BF16) for c in range(3)], axis=1)
        dwide[...] = dwide[...] + dot_nt(low, weights)
        for at, made in ((1, [1, 2]), (3, [3]), (5, [4, 5])):
            @pl.when(q == at)
            def _():
                for n in made:
                    mp_copy(2 * groups + n).start()

    def input_grad():
        gain = gain_ref[...].astype(F32)

        def step(block, sums):
            rows = pl.ds(pl.multiple_of(block * BLOCK, BLOCK), BLOCK)
            normal, inverse = norm_parts(x[rows].astype(F32))
            up = dwide[rows]
            first[rows] = first[rows] + norm_back(up, normal, inverse, gain)
            return (
                sums[0] + jnp.sum(up * normal, axis=0, keepdims=True),
                sums[1] + jnp.sum(up, axis=0, keepdims=True),
            )

        gain_sum, shift_sum = lax.fori_loop(0, BIN // BLOCK, step, (jnp.zeros((1, model), F32),) * 2)
        for half in range(2):
            vec[half, 0:1] = gain_sum
            vec[half, 1:2] = shift_sum

    def ig_copies():
        local = pltpu.make_async_copy(first, ig_ref.at[my_rows], igsem.at[0])
        remote = pltpu.make_async_remote_copy(
            first, ig_ref.at[my_rows], igsem.at[1], igsem.at[2],
            device_id=(dp, 1 - mp), device_id_type=MESH,
        )
        return local, remote

    def vec_copy(n):
        if n == 0:
            src, device = vec.at[1], (dp, 1 - mp)
        else:
            src, device = vec.at[0], (partner[n - 1], mp)
        return pltpu.make_async_remote_copy(
            src, vrecv.at[n], vsem.at[0, n], vsem.at[1, n], device_id=device, device_id_type=MESH
        )

    begin_layer()

    def tick(t, carry):
        ring_tick(t)

        @pl.when(t < middle_tick)
        def _():
            hidden_half(t)

        @pl.when(t == middle_tick)
        def _():
            middle_back()

        @pl.when((t >= attend_tick) & (t < input_tick))
        def _():
            attend_half(t - attend_tick)

        @pl.when(t == input_tick)
        def _():
            input_grad()
            for item in ig_copies():
                item.start()
            vec_copy(0).start()

        for n in range(bits + 1):
            @pl.when(t == input_tick + 1 + n)
            def _():
                vec_copy(n).wait()
                vec[0] = vec[0] + vrecv[n]
                if n < bits:
                    vec_copy(n + 1).start()

        c, valid = at_stage(t, offsets[stages] + 1)

        @pl.when(valid)
        def _():
            write(c, False)

        return carry

    lax.fori_loop(0, ticks, tick, 0)
    for item in ig_copies() + sum_copies():
        item.wait()
    vo_ref[...] = vec[0]


def back(bits, arrays, row, gain, vec_in, bfc, sizes):
    pairs, hidden, model = sizes
    width = pairs * PAIR
    groups = hidden // CHUNK
    chunks = 3 * groups
    plans = color_plans(bits, 0)
    stages = len(plans[0])
    recv = [
        [pltpu.VMEM((SLOTS, size, model // 3), F32) for _, size, kind in plan if kind < 2]
        for plan in plans
    ]
    here = pl.BlockSpec(memory_space=pl.ANY)
    vmem = pl.BlockSpec(memory_space=pltpu.VMEM)
    dma = pltpu.SemaphoreType.DMA
    return pl.pallas_call(
        functools.partial(back_kernel, bits, groups),
        out_shape=[
            jax.ShapeDtypeStruct((hidden, model), F32),
            jax.ShapeDtypeStruct((model, hidden), F32),
            jax.ShapeDtypeStruct((width, model), F32),
            jax.ShapeDtypeStruct((3, model, width), F32),
            jax.ShapeDtypeStruct((2 * BIN, model), F32),
            jax.ShapeDtypeStruct((2 * BIN, model), F32),
            jax.ShapeDtypeStruct((16, model), F32),
        ],
        in_specs=[here] * len(arrays) + [vmem] * 4,
        out_specs=[here] * 6 + [vmem],
        scratch_shapes=[
            pltpu.VMEM((chunks + SENDS, CHUNK, model), F32),
            pltpu.VMEM((LANDS, CHUNK, model), F32),
            recv,
            pltpu.VMEM((2 * pairs, 3, BIN, PAIR), BF16),
            pltpu.VMEM((2 * pairs, BIN, PAIR), BF16),
            pltpu.VMEM((2 * pairs, BIN, PAIR), BF16),
            pltpu.VMEM((BIN, model), BF16),
            pltpu.VMEM((BIN, model), BF16),
            pltpu.VMEM((BIN, model), BF16),
            pltpu.VMEM((model, BIN), BF16),
            pltpu.VMEM((BIN, model), F32),
            pltpu.VMEM((BIN, model), F32),
            pltpu.VMEM((BIN, model), F32),
            pltpu.VMEM((2, model, CHUNK), F32),
            pltpu.VMEM((2, CHUNK, model), F32),
            pltpu.VMEM((2, width, model), F32),
            pltpu.VMEM((2, 3, model, PAIR), F32),
            pltpu.VMEM((BIN, CHUNK), BF16),
            pltpu.VMEM((BIN, CHUNK), BF16),
            pltpu.VMEM((2 * pairs, 8, BIN), F32),
            pltpu.VMEM((BIN, PAIR), F32),
            pltpu.VMEM((BIN, PAIR), F32),
            pltpu.VMEM((2, 16, model), F32),
            pltpu.VMEM((bits + 1, 16, model), F32),
            dma((SLOTS, 3, stages)),
            dma((SLOTS, 3, stages)),
            dma((LANDS,)),
            dma((LANDS,)),
            dma((SLOTS, 12)),
            dma((10,)),
            dma((2, 2)),
            dma((2, 3)),
            dma((6,)),
            dma((2, bits + 1)),
        ],
        compiler_params=pltpu.CompilerParams(
            collective_id=0, has_side_effects=True, vmem_limit_bytes=67_043_328
        ),
        name="back",
    )(*arrays, row, gain, vec_in, bfc)


def on_device(
    tokens, segments, lengths, ln1_gain, ln1_bias, w_qkv, b_qv, w_out, out_bias,
    ln2_gain, ln2_bias, w_fc, b_fc, w_proj, proj_bias, cotangent,
):
    model = tokens.shape[1]
    width = w_qkv.shape[2]
    hidden = w_fc.shape[1]
    pairs = width // PAIR
    groups = lax.axis_size("dp")
    bits = groups.bit_length() - 1
    if lax.axis_size("mp") != 2 or groups != 1 << bits or tokens.shape[0] != 2 * BIN:
        raise ValueError("unsupported mesh")
    side = lax.axis_index("mp")
    mine = side.astype(jnp.int32).reshape(1)
    swap = [(0, 1), (1, 0)]

    def cross(value):
        return lax.ppermute(value, "mp", swap)

    w3 = jnp.transpose(w_qkv, (1, 0, 2)).astype(F32)
    small = jnp.concatenate([b_qv.reshape(-1), b_fc]).astype(F32)
    small_other = cross(small)
    w3_other = cross(w3)
    wo_own, wf_own, wp_own = (item.astype(F32) for item in (w_out, w_fc, w_proj))
    wo_other = cross(wo_own)
    wf_other = cross(wf_own)
    wp_other = cross(wp_own)

    def qkv_bias(flat):
        return jnp.stack([flat[:width], jnp.zeros((width,), F32), flat[width : 2 * width]])

    own, other_front = front(
        mine, tokens, segments.reshape(2, BIN), lengths,
        ln1_gain.reshape(1, -1), ln1_bias.reshape(1, -1), w3, qkv_bias(small), width,
    )
    qkv_own, attn_own, lse_own, h1, start, row = own
    small_other, w3_other, h1 = lax.optimization_barrier((small_other, w3_other, h1))
    qkv_other, attn_other, lse_other = other_front(h1, start, w3_other, qkv_bias(small_other))
    vec_in = jnp.stack([out_bias, ln2_gain, ln2_bias, proj_bias]).astype(F32)
    bfc = jnp.concatenate([small[2 * width :], small_other[2 * width :]]).reshape(-1, CHUNK)
    arrays = (
        qkv_own, qkv_other, attn_own, attn_other, h1, w3, w3_other, tokens, cotangent,
        wo_own, wo_other, wf_own, wf_other, wp_own, wp_other, lse_own, lse_other,
    )
    grad_proj, grad_fc, grad_out, grad_qkv, input_grad, block_sum, rows = back(
        bits, arrays, row, ln1_gain.reshape(1, -1), vec_in, bfc, (pairs, hidden, model)
    )
    block_out = (block_sum + vec_in[3]).astype(BF16)
    grad_qkv = jnp.transpose(grad_qkv, (1, 0, 2))
    return (
        block_out,
        input_grad,
        rows[0],
        rows[1],
        grad_qkv,
        rows[8].reshape(2, width),
        grad_out,
        rows[2],
        rows[3],
        rows[4],
        grad_fc,
        rows[6:8].reshape(-1),
        grad_proj,
        rows[5],
    )


def solution(mesh):
    rows = P("dp", None)
    placed = (
        rows, P("dp"), rows, P(), P(), P(None, None, "mp"), P(None, "mp"), P("mp", None), P(),
        P(), P(), P(None, "mp"), P("mp"), P("mp", None), P(), rows,
    )
    results = (
        rows, rows, P(), P(), P(None, None, "mp"), P(None, "mp"), P("mp", None), P(), P(), P(),
        P(None, "mp"), P("mp"), P("mp", None), P(),
    )
    return jax.shard_map(
        on_device, mesh=mesh, in_specs=placed, out_specs=results, check_vma=False
    )
```

profile of v0, /device:TPU:0, one launch (start us, length us, event | category | flops | bytes accessed | tf_op | source)
XLA Modules:
  0.0 309.9 jit_solution(16681389695213364113)
XLA Ops:
  0.7 4.6 %convert_element_type.29.wf_own_ref = f32[768,1536]{1,0:T(8,128)} convert(bf16[768,1536]{1,0:T(8,128)(2,1)} %param.27) | non-fusion elementwise | flops 1179648 | bytes 7077888 | tf_op jit(solution)/shard_map/convert_element_type | solution.py:820
  5.3 0.5 collective-permute-start.3
  5.8 2.5 convert_element_type.30.wp_own_ref
  8.4 0.0 copy-start.10
  8.4 0.0 copy-start.12
  8.4 0.0 copy-start.13
  8.4 0.0 copy-start.14
  8.4 0.0 copy-start.15
  8.4 0.0 copy-start.16
  8.4 0.1 collective-permute-start.4
  8.5 2.0 convert_bitcast_fusion.w_ref.w3_own_ref
  10.5 0.5 collective-permute-start.1
  11.1 0.1 collective-permute-start
  11.2 0.1 convert_element_type.28.wo_own_ref
  11.2 0.0 copy-start.1
  11.3 0.5 collective-permute-start.2
  11.8 0.6 reshape.67.gain_ref
  12.4 0.6 reshape.66.seg_ref
  13.0 0.6 reshape.68.shift_ref
  13.6 0.0 copy-done.14
  13.7 0.1 pad.10.clone
  13.8 0.7 pad_maximum_fusion.1.bias_ref
  14.5 20.4 %own_front.1 = (bf16[3,3,1024,128]{3,2,1,0:T(8,128)(2,1)}, bf16[3,1024,128]{2,1,0:T(8,128)(2,1)}, f32[3,8,1024]{2,1,0:T(8,128)}, bf16[1024,768]{1,0:T(8,128)(2,1...) custom-call(s32[1]{0:T(128)} %bitcast.mp_ref, bf16[2048,768]{1,0:T(8,128)(2,1)} %x_ref.3, s32[2,1024]{1,0:T(2,128)} %reshape.66.seg_ref, ...), custom_call_target="tpu_custom_call" | custom-call | flops 6000000000 | bytes 10000000 | tf_op jit(solution)/shard_map/own_front/pallas_call | solution.py:201
  34.8 0.6 slice_reduce_fusion
  35.4 0.0 collective-permute-done
  35.4 0.0 collective-permute-done.1.w_ref.w3_other_ref
  35.5 0.6 pad_maximum_fusion.bfc_ref
  36.1 0.7 pad_maximum_fusion.2.bias_ref
  36.8 18.8 %other_front.1 = (bf16[3,3,1024,128]{3,2,1,0:T(8,128)(2,1)}, bf16[3,1024,128]{2,1,0:T(8,128)(2,1)}, f32[3,8,1024]{2,1,0:T(8,128)}) custom-call(bf16[1024,768]{1,0:T(8,128)(2,1)} %get-tuple-element.35.h1_ref, s32[1024,1]{1,0:T(8,128)} %get-tuple-element.36.start_ref, f32[3,768,384]{2,1,0:T(8,128)} %collective-permute-done.1.w_ref.w3_other_ref, ...), custom_call_target="tpu_custom_call" | custom-call | flops 6000000000 | bytes 10000000 | tf_op jit(solution)/shard_map/other_front/pallas_call | solution.py:190
  55.5 0.0 collective-permute-done.2.wo_other_ref
  55.5 1.1 copy-done.5
  56.6 0.0 collective-permute-done.3.wf_other_ref
  56.6 0.0 collective-permute-done.4.wp_other_ref
  56.6 230.6 %back.1 = (f32[1536,768]{1,0:T(8,128)}, f32[768,1536]{1,0:T(8,128)}, f32[384,768]{1,0:T(8,128)}, f32[3,768,384]{2,1,0:T(8,128)}, f32[2048,768]{1,0:T(8,128)}, /*index=5*/f32[2048,768]{1,0:T(8,128)}, f32[16,768]{1,0:T(8,128)}) custom-call(bf16[3,3,1024,128]{3,2,1,0:T(8,128)(2,1)} %get-tuple-element.33.qkv_own_ref, ...), custom_call_target="tpu_custom_call" | custom-call | tf_op jit(solution)/shard_map/back/pallas_call | solution.py:741
  287.2 1.7 slice_reduce_fusion.1
  288.9 0.7 slice.77
  289.7 0.6 reshape_squeeze.3
  290.3 0.6 reshape.70
  290.9 5.1 %add_convert_fusion = bf16[2048,768]{1,0:T(8,128)(2,1)} fusion(f32[2048,768]{1,0:T(8,128)} %get-tuple-element.45, f32[768]{0:T(1024)} %slice_reduce_fusion), kind=kLoop, calls=%fused_computation | loop fusion | flops 3145728 | bytes 9440256 | tf_op jit(solution)/shard_map/convert_element_type | solution.py:844
  296.0 3.2 %copy.35 = f32[2048,768]{1,0:T(8,128)} copy(f32[2048,768]{1,0:T(8,128)S(1)} %copy-done) | data formatting | bytes 12582912
  299.2 1.8 copy-done.2
  301.0 1.8 copy.36
  302.8 0.3 copy-done.6
  303.1 1.0 copy.37
  304.1 2.4 copy.38
  306.5 0.8 slice-done
  307.3 0.3 slice-done.1
  307.7 2.2 copy.39
  (49 shorter events, 0.2 us)
Async XLA Ops:
  0.6 5.2 %copy-start.3 = (bf16[1536,768]{1,0:T(8,128)(2,1)S(1)}, bf16[1536,768]{1,0:T(8,128)(2,1)}, u32[]{:S(2)}) copy-start(bf16[1536,768]{1,0:T(8,128)(2,1)} %param.29) | copy-start | bytes 7077892
  5.3 3.2 %copy-start.4 = (bf16[768,3,384]{2,0,1:T(8,128)(2,1)S(1)}, bf16[768,3,384]{2,0,1:T(8,128)(2,1)}, u32[]{:S(2)}) copy-start(bf16[768,3,384]{2,0,1:T(8,128)(2,1)} %param.21) | copy-start | bytes 5308420
  5.3 51.3 %collective-permute-start.3 = (f32[768,1536]{1,0:T(8,128)}, f32[768,1536]{1,0:T(8,128)}, u32[]{:S(2)}, u32[]{:S(2)}) collective-permute-start(f32[768,1536]{1,0:T(8,128)} %convert_element_type.29.wf_own_ref), channel_id=1, source_target_pairs={{0,1},{1,0},{2,3},{3,2},{4,5},{5,4},{6,7},{7,6},{8,9},{9,8},{10,11... | collective-permute-start | bytes 14155784 | tf_op jit(solution)/shard_map/ppermute | solution.py:814
  8.3 2.7 copy-start.17
  8.3 2.7 copy-start.9
  8.3 2.8 copy-start.7
  8.4 3.5 %copy-start.11 = (bf16[768]{0:T(1024)(128)(2,1)S(1)}, bf16[768]{0:T(1024)(128)(2,1)}, u32[]{:S(2)}) copy-start(bf16[768]{0:T(1024)(128)(2,1)} %param.19) | copy-start | bytes 4612
  8.4 4.1 %copy-start.10 = (s32[2048]{0:T(1024)S(1)}, s32[2048]{0:T(1024)}, u32[]{:S(2)}) copy-start(s32[2048]{0:T(1024)} %param.17) | copy-start | bytes 24580
  8.4 4.7 %copy-start.12 = (bf16[768]{0:T(1024)(128)(2,1)S(1)}, bf16[768]{0:T(1024)(128)(2,1)}, u32[]{:S(2)}) copy-start(bf16[768]{0:T(1024)(128)(2,1)} %param.20) | copy-start | bytes 4612
  8.4 5.2 %copy-start.13 = (bf16[768]{0:T(1024)(128)(2,1)S(1)}, bf16[768]{0:T(1024)(128)(2,1)}, u32[]{:S(2)}) copy-start(bf16[768]{0:T(1024)(128)(2,1)} %param.24) | copy-start | bytes 4612
  8.4 5.2 %copy-start.14 = (bf16[768]{0:T(1024)(128)(2,1)S(1)}, bf16[768]{0:T(1024)(128)(2,1)}, u32[]{:S(2)}) copy-start(bf16[768]{0:T(1024)(128)(2,1)} %param.25) | copy-start | bytes 4612
  8.4 5.2 %copy-start.15 = (bf16[768]{0:T(1024)(128)(2,1)S(1)}, bf16[768]{0:T(1024)(128)(2,1)}, u32[]{:S(2)}) copy-start(bf16[768]{0:T(1024)(128)(2,1)} %param.26) | copy-start | bytes 4612
  8.4 5.2 %copy-start.16 = (bf16[768]{0:T(1024)(128)(2,1)S(1)}, bf16[768]{0:T(1024)(128)(2,1)}, u32[]{:S(2)}) copy-start(bf16[768]{0:T(1024)(128)(2,1)} %param.30) | copy-start | bytes 4612
  8.4 48.2 %collective-permute-start.4 = (f32[1536,768]{1,0:T(8,128)}, f32[1536,768]{1,0:T(8,128)}, u32[]{:S(2)}, u32[]{:S(2)}) collective-permute-start(f32[1536,768]{1,0:T(8,128)} %convert_element_type.30.wp_own_ref), channel_id=1, source_target_pairs={{0,1},{1,0},{2,3},{3,2},{4,5},{5,4},{6,7},{7,6},{8,9},{9,8},{10,11... | collective-permute-start | bytes 14155784 | tf_op jit(solution)/shard_map/ppermute | solution.py:814
  10.5 24.9 %collective-permute-start.1 = (f32[3,768,384]{2,1,0:T(8,128)}, f32[3,768,384]{2,1,0:T(8,128)}, u32[]{:S(2)}, u32[]{:S(2)}) collective-permute-start(f32[3,768,384]{2,1,0:T(8,128)} %convert_bitcast_fusion.w_ref.w3_own_ref), channel_id=1, source_target_pairs={{0,1},{1,0},{2,3},{3,2},{4,5},{5,4},{6,7},{7,6},{8,9},{9,8},{10,11... | collective-permute-start | bytes 10616840 | tf_op jit(solution)/shard_map/ppermute | solution.py:814
  11.1 24.4 %collective-permute-start = (f32[2304]{0:T(1024)S(1)}, f32[2304]{0:T(1024)S(1)}, u32[]{:S(2)}, u32[]{:S(2)}) collective-permute-start(f32[2304]{0:T(1024)S(1)} %maximum_convert_fusion), channel_id=1, source_target_pairs={{0,1},{1,0},{2,3},{3,2},{4,5},{5,4},{6,7},{7,6},{8,9},{9,8},{10,11... | collective-permute-start | bytes 27656 | tf_op jit(solution)/shard_map/ppermute | solution.py:814
  11.2 23.6 %copy-start.1 = (f32[384,768]{1,0:T(8,128)}, f32[384,768]{1,0:T(8,128)S(1)}, u32[]{:S(2)}) copy-start(f32[384,768]{1,0:T(8,128)S(1)} %convert_element_type.28.wo_own_ref) | copy-start | bytes 3538948
  11.3 44.3 %collective-permute-start.2 = (f32[384,768]{1,0:T(8,128)S(1)}, f32[384,768]{1,0:T(8,128)S(1)}, u32[]{:S(2)}, u32[]{:S(2)}) collective-permute-start(f32[384,768]{1,0:T(8,128)S(1)} %convert_element_type.28.wo_own_ref), channel_id=1, source_target_pairs={{0,1},{1,0},{2,3},{3,2},{4,5},{5,4},{6,7},{7,6},{8,9},{9,8},{10,11... | collective-permute-start | bytes 3538952 | tf_op jit(solution)/shard_map/ppermute | solution.py:814
  13.8 21.0 %copy-start.8 = (f32[4,768]{1,0:T(4,128)}, f32[4,768]{1,0:T(4,128)S(1)}, u32[]{:S(2)}) copy-start(f32[4,768]{1,0:T(4,128)S(1)} %maximum_convert_fusion.1.vec_in_ref) | copy-start | bytes 36868
  55.5 1.1 copy-start.5
  290.9 5.1 %copy-start = (f32[2048,768]{1,0:T(8,128)S(1)}, f32[2048,768]{1,0:T(8,128)}, u32[]{:S(2)}) copy-start(f32[2048,768]{1,0:T(8,128)} %get-tuple-element.78) | copy-start | bytes 18874372
  290.9 13.3 %slice-start.2 = ((s8[4718592]{0:T(1024)(128)(4,1)}), s8[4194304]{0:T(1024)(128)(4,1)S(1)}, s32[]{:S(2)}) async-start(s8[4718592]{0:T(1024)(128)(4,1)} %bitcast.7), calls=%async_computation.2 | async-start | bytes 8388608
  296.0 5.0 %copy-start.2 = (f32[3,768,384]{2,1,0:T(8,128)S(1)}, f32[3,768,384]{2,1,0:T(8,128)}, u32[]{:S(2)}) copy-start(f32[3,768,384]{2,1,0:T(8,128)} %get-tuple-element.48) | copy-start | bytes 10616836
  296.0 8.1 %slice-start.3 = ((s8[4718592]{0:T(1024)(128)(4,1)}), s8[524288]{0:T(1024)(128)(4,1)S(1)}, s32[]{:S(2)}) async-start(s8[4718592]{0:T(1024)(128)(4,1)} %bitcast.7), calls=%async_computation.3 | async-start | bytes 1048576
  301.0 2.1 copy-start.6
  303.1 4.2 %slice-start = ((s8[4718592]{0:T(1024)(128)(4,1)}), s8[4194304]{0:T(1024)(128)(4,1)S(1)}, s32[]{:S(2)}) async-start(s8[4718592]{0:T(1024)(128)(4,1)} %bitcast.5), calls=%async_computation | async-start | bytes 8388608
  304.1 3.5 %slice-start.1 = ((s8[4718592]{0:T(1024)(128)(4,1)}), s8[524288]{0:T(1024)(128)(4,1)S(1)}, s32[]{:S(2)}) async-start(s8[4718592]{0:T(1024)(128)(4,1)} %bitcast.5), calls=%async_computation.1 | async-start | bytes 1048576
where the time goes:
time: 310 us
  Pallas kernels  270 us (87%)
  local copies, waits for them, and re-layouts  21.2 us (7%)
  other arithmetic  16.4 us (5%)
    pallas_call x1, Pallas kernels, back(): pl.pallas_call(functools.partial(back_kernel, bits, groups), out_shape=[j...  231 us
    pallas_call x1, Pallas kernels, front(): return (own(mine, x, seg, lens, gain, shift, w_own, bias_own), other)  20.4 us
    pallas_call x1, Pallas kernels, other(): pl.pallas_call(other_front_kernel, out_shape=out_shapes, grid=(pairs,), i...  18.8 us
    unnamed x49, local copies, waits for them, and re-layouts  15 us
    convert_element_type x3, other arithmetic, on_device(): item.astype(F32)  7.27 us
  transfers between devices with their start and end apart: 5, of which 0 were waited for; matrix products, arithmetic and copies ran while one was open for 3% of the time, Pallas kernels for 13%

commit v1 on v0

--- a/solution.py
+++ b/solution.py
@@ -15,6 +15,8 @@
 SLOTS = 4
 SENDS = 4
 LANDS = 5
+QV_ROW = 6
+FC_ROW = 7
 
 epsilon = 1e-05
 gelu_scale = 0.7978845608028654
@@ -95,21 +97,26 @@
         attn_ref[0, rows] = jnp.where(lane < HEAD_DIM, mixed[0], mixed[1]).astype(BF16)
 
 
-def project_and_attend(h1, w_ref, bias_ref, start_ref, qkv_ref, attn_ref, lse_ref):
+def project_and_attend(h1, w_ref, pack_ref, start_ref, qkv_ref, attn_ref, lse_ref):
+    width = pl.num_programs(0) * PAIR
+    place = pl.program_id(0) * PAIR
     for c in range(3):
-        out = dot_nn(h1, w_ref[c].astype(BF16)) + bias_ref[c : c + 1]
+        out = dot_nn(h1, w_ref[c].astype(BF16))
+        if c != 1:
+            at = place if c == 0 else width + place
+            out = out + pack_ref[QV_ROW : QV_ROW + 1, pl.ds(pl.multiple_of(at, PAIR), PAIR)]
         qkv_ref[0, c] = out.astype(BF16)
     attend_pair(qkv_ref, start_ref, attn_ref, lse_ref)
 
 
 def own_front_kernel(
-    mp_ref, x_ref, seg_ref, len_ref, gain_ref, shift_ref, w_ref, bias_ref,
+    mp_ref, x_ref, seg_ref, len_ref, pack_ref, w_ref,
     qkv_ref, attn_ref, lse_ref, h1_ref, start_ref, row_ref,
 ):
     @pl.when(pl.program_id(0) == 0)
     def _():
-        gain = gain_ref[...].astype(F32)
-        shift = shift_ref[...].astype(F32)
+        gain = pack_ref[0:1]
+        shift = pack_ref[1:2]
         for block in range(BIN // BLOCK):
             rows = slice(block * BLOCK, (block + 1) * BLOCK)
             normal, _ = norm_parts(x_ref[rows].astype(F32))
@@ -128,24 +135,21 @@
         start_ref[...] = start.astype(jnp.int32)
         row_ref[...] = column_to_row(start).astype(jnp.int32)
 
-    project_and_attend(h1_ref[...], w_ref, bias_ref, start_ref, qkv_ref, attn_ref, lse_ref)
-
-
-def other_front_kernel(h1_ref, start_ref, w_ref, bias_ref, qkv_ref, attn_ref, lse_ref):
-    project_and_attend(h1_ref[...], w_ref, bias_ref, start_ref, qkv_ref, attn_ref, lse_ref)
+    project_and_attend(h1_ref[...], w_ref, pack_ref, start_ref, qkv_ref, attn_ref, lse_ref)
+
+
+def other_front_kernel(h1_ref, start_ref, pack_ref, w_ref, qkv_ref, attn_ref, lse_ref):
+    project_and_attend(h1_ref[...], w_ref, pack_ref, start_ref, qkv_ref, attn_ref, lse_ref)
 
 
 def fixed(shape):
     return pl.BlockSpec(shape, lambda *_: (0,) * len(shape), pipeline_mode=pl.Buffered(1))
 
 
-def front(mine, x, seg, lens, gain, shift, w_own, bias_own, width):
+def front(mine, x, seg, lens, pack, w_own, width):
     model = x.shape[1]
     pairs = width // PAIR
-    per_pair = [
-        pl.BlockSpec((3, model, PAIR), lambda p, *_: (0, 0, p)),
-        pl.BlockSpec((3, PAIR), lambda p, *_: (0, p)),
-    ]
+    per_pair = [pl.BlockSpec((3, model, PAIR), lambda p, *_: (0, 0, p))]
     outs = [
         pl.BlockSpec((1, 3, BIN, PAIR), lambda p, *_: (p, 0, 0, 0)),
         pl.BlockSpec((1, BIN, PAIR), lambda p, *_: (p, 0, 0)),
@@ -171,7 +175,7 @@
             grid=(pairs,),
             in_specs=[
                 pl.BlockSpec((BIN, model), lambda p, m: (m[0], 0)),
-                fixed(seg.shape), fixed(lens.shape), fixed((1, model)), fixed((1, model)),
+                fixed(seg.shape), fixed(lens.shape), fixed(pack.shape),
             ]
             + per_pair,
             out_specs=outs
@@ -186,19 +190,19 @@
         name="own_front",
     )
 
-    def other(h1, start, w_other, bias_other):
+    def other(h1, start, pack_other, w_other):
         return pl.pallas_call(
             other_front_kernel,
             out_shape=out_shapes,
             grid=(pairs,),
-            in_specs=[fixed((BIN, model)), fixed((BIN, 1))] + per_pair,
+            in_specs=[fixed((BIN, model)), fixed((BIN, 1)), fixed(pack.shape)] + per_pair,
             out_specs=outs,
             compiler_params=params,
             cost_estimate=cost,
             name="other_front",
-        )(h1, start, w_other, bias_other)
-
-    return own(mine, x, seg, lens, gain, shift, w_own, bias_own), other
+        )(h1, start, pack_other, w_other)
+
+    return own(mine, x, seg, lens, pack, w_own), other
 
 
 def halving_plan(order, rows):
@@ -271,12 +275,12 @@
 def back_kernel(
     bits, groups,
     qkv_own_ref, qkv_other_ref, attn_own_ref, attn_other_ref, h1_ref, w3_own_ref, w3_other_ref,
-    x_ref, cot_ref, wo_own_ref, wo_other_ref, wf_own_ref, wf_other_ref, wp_own_ref, wp_other_ref,
-    lse_own_ref, lse_other_ref, row_ref, gain_ref, vec_in_ref, bfc_ref,
-    op_ref, of_ref, oa_ref, oq_ref, ig_ref, sum_ref, vo_ref,
+    x_ref, cot_ref, wo_own_ref, wo_other_ref, wf_ref, wp_ref,
+    lse_own_ref, lse_other_ref, row_ref, pack_ref, pack_other_ref,
+    op_ref, of_ref, oa_ref, oq_ref, ig_ref, bo_ref, sum_ref, vo_ref,
     acc, mpbuf, rbufs, qkv, dattn, attn, cot, x, tall, flip, total, dwide, first,
-    wf, wp, wo, w3, act, slope, lse, dk, dv, vec, vrecv,
-    ssem, rsem, mps, mpr, wsem, lsem, bsem, hsem, igsem, vsem,
+    wf, wp, wf_low, wp_low, wf_out, wp_out, wo, w3, act, slope, lse, dk, dv, vec, vrecv,
+    ssem, rsem, mps, mpr, wsem, lsem, bsem, wsend, wrecv, hsem, igsem, vsem,
 ):
     dp = lax.axis_index("dp")
     mp = lax.axis_index("mp")
@@ -293,6 +297,7 @@
     pieces = model // CHUNK
 
     my_rows = pl.ds(pl.multiple_of(mp * BIN, BIN), BIN)
+    far_rows = pl.ds(pl.multiple_of((1 - mp) * BIN, BIN), BIN)
     loads = []
 
     def load(src, dst):
@@ -303,24 +308,38 @@
     load(wo_own_ref, wo.at[0])
     load(wo_other_ref, wo.at[1])
     load(x_ref.at[my_rows], x)
+    early = len(loads)
     load(cot_ref.at[my_rows], cot)
-    early = len(loads)
     load(qkv_own_ref, qkv.at[0:pairs])
     load(qkv_other_ref, qkv.at[pairs : 2 * pairs])
     load(lse_own_ref, lse.at[0:pairs])
     load(lse_other_ref, lse.at[pairs : 2 * pairs])
 
-    def block_loads(u, begin):
-        slot = u % 2
-        at = pl.ds(pl.multiple_of((u // 2) * CHUNK, CHUNK), CHUNK)
-        for half, fc_ref, proj_ref in ((0, wf_own_ref, wp_own_ref), (1, wf_other_ref, wp_other_ref)):
-            @pl.when(slot == half)
-            def _():
-                for item in (
-                    pltpu.make_async_copy(fc_ref.at[:, at], wf.at[half], bsem.at[half, 0]),
-                    pltpu.make_async_copy(proj_ref.at[at], wp.at[half], bsem.at[half, 1]),
-                ):
-                    item.start() if begin else item.wait()
+    def block_loads(b):
+        slot = b % 2
+        at = pl.ds(pl.multiple_of(b * CHUNK, CHUNK), CHUNK)
+        return [
+            pltpu.make_async_copy(wf_ref.at[:, at], wf_low.at[slot], bsem.at[slot, 0]),
+            pltpu.make_async_copy(wp_ref.at[at], wp_low.at[slot], bsem.at[slot, 1]),
+        ]
+
+    def block_sends(b):
+        slot = b % 2
+        return [
+            pltpu.make_async_remote_copy(
+                src, dst.at[slot], wsend.at[n], wrecv.at[slot, n],
+                device_id=(dp, 1 - mp), device_id_type=MESH,
+            )
+            for n, (src, dst) in enumerate(((wf_out, wf), (wp_out, wp)))
+        ]
+
+    def send_block(b):
+        for item in block_loads(b):
+            item.wait()
+        wf_out[...] = wf_low[b % 2].astype(F32)
+        wp_out[...] = wp_low[b % 2].astype(F32)
+        for item in block_sends(b):
+            item.start()
 
     def w3_loads(q, begin):
         slot = q % 2
@@ -337,7 +356,9 @@
 
     for item in loads:
         item.start()
-    block_loads(jnp.int32(0), True)
+    for b in range(2):
+        for item in block_loads(b):
+            item.start()
 
     barrier = pltpu.get_barrier_semaphore()
     for b in range(bits):
@@ -502,11 +523,13 @@
                         copy(c, color, s + 1).start()
 
     def begin_layer():
+        send_block(0)
         for item in loads[:early]:
             item.wait()
-        out_bias = vec_in_ref[0:1]
-        gain = vec_in_ref[1:2]
-        shift = vec_in_ref[2:3]
+        out_bias = pack_ref[2:3]
+        gain = pack_ref[3:4]
+        shift = pack_ref[4:5]
+        proj_bias = pack_ref[5:6]
         vec[...] = jnp.zeros_like(vec)
 
         def step(block, carry):
@@ -517,7 +540,7 @@
                 branch = branch + dot_nn(jnp.concatenate(mixed, axis=1), wo[half].astype(BF16))
             r1 = x[rows].astype(F32) + branch
             first[rows] = r1
-            total[rows] = r1
+            total[rows] = r1 + proj_bias
             dwide[rows] = jnp.zeros((BLOCK, model), F32)
             normal, _ = norm_parts(r1)
             h2 = (normal * gain + shift).astype(BF16)
@@ -526,38 +549,53 @@
             return carry
 
         lax.fori_loop(0, BIN // BLOCK, step, 0)
+        loads[early].wait()
 
     def hidden_half(u):
         b, half = u // 2, u % 2
-        block_loads(u, False)
-
-        @pl.when(u + 1 < 2 * groups)
-        def _():
-            block_loads(u + 1, True)
+
+        @pl.when(half == 1)
+        def _():
+            for item in block_sends(b):
+                item.wait()
+
+            @pl.when(b + 1 < groups)
+            def _():
+                send_block(b + 1)
+
+            @pl.when(b + 2 < groups)
+            def _():
+                for item in block_loads(b + 2):
+                    item.start()
+
+            wf_low[2] = wf[b % 2].astype(BF16)
+            wp_low[2] = wp[b % 2].astype(BF16)
 
         span = 2 * BLOCK
-        wf_low = wf[half].astype(BF16)
-        wp_low = wp[half].astype(BF16)
-        bias = bfc_ref[pl.ds(half * groups + b, 1), :]
+        place = jnp.where(half == 0, b % 2, 2)
+        fc = wf_low[place]
+        proj = wp_low[place]
+        at = pl.ds(FC_ROW + b // pieces, 1), pl.ds(pl.multiple_of((b % pieces) * CHUNK, CHUNK), CHUNK)
+        bias = jnp.where(half == 0, pack_ref[at], pack_other_ref[at])
         df_sum = jnp.zeros((1, CHUNK), F32)
         for block in range(BIN // span):
             rows = slice(block * span, (block + 1) * span)
-            pre = dot_nn(tall[rows], wf_low) + bias
+            pre = dot_nn(tall[rows], fc) + bias
             hidden, rise = gelu_pair(pre)
             hidden = hidden.astype(BF16)
             act[rows] = hidden
-            total[rows] = total[rows] + dot_nn(hidden, wp_low)
-            df = (dot_nt(cot[rows], wp_low) * rise).astype(BF16)
+            total[rows] = total[rows] + dot_nn(hidden, proj)
+            df = (dot_nt(cot[rows], proj) * rise).astype(BF16)
             slope[rows] = df
             df_sum = df_sum + jnp.sum(df.astype(F32), axis=0, keepdims=True)
-            dwide[rows] = dwide[rows] + dot_nt(df, wf_low)
+            dwide[rows] = dwide[rows] + dot_nt(df, fc)
 
         vec[half, pl.ds(6 + b // pieces, 1), pl.ds(pl.multiple_of((b % pieces) * CHUNK, CHUNK), CHUNK)] = df_sum
         at = jnp.where(half == 0, 2 * b, chunks + (2 * b) % SENDS)
         acc[at] = dot_tn(act[...], cot[...])
-        fc = dot_nn(flip[...], slope[...])
+        grad = dot_nn(flip[...], slope[...])
         for n in range(pieces):
-            acc[at + 1, :, n * CHUNK : (n + 1) * CHUNK] = fc[n * CHUNK : (n + 1) * CHUNK]
+            acc[at + 1, :, n * CHUNK : (n + 1) * CHUNK] = grad[n * CHUNK : (n + 1) * CHUNK]
 
         @pl.when(half == 1)
         def _():
@@ -570,18 +608,32 @@
         rows = pl.ds(pl.multiple_of((piece % 2) * PAIR, PAIR), PAIR)
         acc[at, rows, part * width : part * width + value.shape[1]] = value
 
-    def sum_copies():
-        local = pltpu.make_async_copy(total, sum_ref.at[my_rows], igsem.at[3])
-        remote = pltpu.make_async_remote_copy(
-            total, sum_ref.at[my_rows], igsem.at[4], igsem.at[5],
+    def sum_copy():
+        return pltpu.make_async_remote_copy(
+            total, sum_ref, igsem.at[3], igsem.at[4],
             device_id=(dp, 1 - mp), device_id_type=MESH,
         )
-        return local, remote
+
+    def sum_loads(part):
+        return [
+            pltpu.make_async_copy(
+                sum_ref.at[(2 * part + n) * CHUNK : (2 * part + n + 1) * CHUNK], wp.at[n], igsem.at[5 + n]
+            )
+            for n in range(2)
+        ]
+
+    def round_far(part):
+        for n, item in enumerate(sum_loads(part)):
+            item.wait()
+            cot[(2 * part + n) * CHUNK : (2 * part + n + 1) * CHUNK] = wp[n].astype(BF16)
+
+    def out_copy(n):
+        src, rows = ((tall, my_rows), (cot, far_rows))[n]
+        return pltpu.make_async_copy(src, bo_ref.at[rows], igsem.at[7 + n])
 
     def middle_back():
-        for item in sum_copies():
-            item.start()
-        gain = vec_in_ref[1:2]
+        sum_copy().start()
+        gain = pack_ref[3:4]
         w3_loads(jnp.int32(0), True)
 
         def step(block, sums):
@@ -613,7 +665,7 @@
                 put_piece(half, piece, 0, grad[piece * PAIR : (piece + 1) * PAIR])
         mp_copy(2 * groups).start()
         h1_load().start()
-        for item in loads[early:]:
+        for item in loads[early + 1 :]:
             item.wait()
 
     def attend_half(q):
@@ -644,7 +696,7 @@
                     mp_copy(2 * groups + n).start()
 
     def input_grad():
-        gain = gain_ref[...].astype(F32)
+        gain = pack_ref[0:1]
 
         def step(block, sums):
             rows = pl.ds(pl.multiple_of(block * BLOCK, BLOCK), BLOCK)
@@ -701,6 +753,25 @@
             for item in ig_copies():
                 item.start()
             vec_copy(0).start()
+            tall[...] = total[...].astype(BF16)
+            out_copy(0).start()
+
+        @pl.when(t == input_tick + 1)
+        def _():
+            sum_copy().wait()
+            for item in sum_loads(0):
+                item.start()
+
+        @pl.when(t == input_tick + 2)
+        def _():
+            round_far(0)
+            for item in sum_loads(1):
+                item.start()
+
+        @pl.when(t == input_tick + 3)
+        def _():
+            round_far(1)
+            out_copy(1).start()
 
         for n in range(bits + 1):
             @pl.when(t == input_tick + 1 + n)
@@ -719,12 +790,12 @@
         return carry
 
     lax.fori_loop(0, ticks, tick, 0)
-    for item in ig_copies() + sum_copies():
+    for item in list(ig_copies()) + [out_copy(0), out_copy(1)]:
         item.wait()
     vo_ref[...] = vec[0]
 
 
-def back(bits, arrays, row, gain, vec_in, bfc, sizes):
+def back(bits, arrays, row, packs, sizes):
     pairs, hidden, model = sizes
     width = pairs * PAIR
     groups = hidden // CHUNK
@@ -746,11 +817,12 @@
             jax.ShapeDtypeStruct((width, model), F32),
             jax.ShapeDtypeStruct((3, model, width), F32),
             jax.ShapeDtypeStruct((2 * BIN, model), F32),
-            jax.ShapeDtypeStruct((2 * BIN, model), F32),
+            jax.ShapeDtypeStruct((2 * BIN, model), BF16),
+            jax.ShapeDtypeStruct((BIN, model), F32),
             jax.ShapeDtypeStruct((16, model), F32),
         ],
-        in_specs=[here] * len(arrays) + [vmem] * 4,
-        out_specs=[here] * 6 + [vmem],
+        in_specs=[here] * len(arrays) + [vmem] * 3,
+        out_specs=[here] * 7 + [vmem],
         scratch_shapes=[
             pltpu.VMEM((chunks + SENDS, CHUNK, model), F32),
             pltpu.VMEM((LANDS, CHUNK, model), F32),
@@ -767,6 +839,10 @@
             pltpu.VMEM((BIN, model), F32),
             pltpu.VMEM((2, model, CHUNK), F32),
             pltpu.VMEM((2, CHUNK, model), F32),
+            pltpu.VMEM((3, model, CHUNK), BF16),
+            pltpu.VMEM((3, CHUNK, model), BF16),
+            pltpu.VMEM((model, CHUNK), F32),
+            pltpu.VMEM((CHUNK, model), F32),
             pltpu.VMEM((2, width, model), F32),
             pltpu.VMEM((2, 3, model, PAIR), F32),
             pltpu.VMEM((BIN, CHUNK), BF16),
@@ -783,15 +859,17 @@
             dma((SLOTS, 12)),
             dma((10,)),
             dma((2, 2)),
+            dma((2,)),
+            dma((2, 2)),
             dma((2, 3)),
-            dma((6,)),
+            dma((9,)),
             dma((2, bits + 1)),
         ],
         compiler_params=pltpu.CompilerParams(
             collective_id=0, has_side_effects=True, vmem_limit_bytes=67_043_328
         ),
         name="back",
-    )(*arrays, row, gain, vec_in, bfc)
+    )(*arrays, row, *packs)
 
 
 def on_device(
@@ -814,34 +892,26 @@
         return lax.ppermute(value, "mp", swap)
 
     w3 = jnp.transpose(w_qkv, (1, 0, 2)).astype(F32)
-    small = jnp.concatenate([b_qv.reshape(-1), b_fc]).astype(F32)
-    small_other = cross(small)
+    vectors = (ln1_gain, ln1_bias, out_bias, ln2_gain, ln2_bias, proj_bias, b_qv.reshape(-1), b_fc)
+    pack = jnp.concatenate([item.astype(F32) for item in vectors]).reshape(-1, model)
+    pack_other = cross(pack)
     w3_other = cross(w3)
-    wo_own, wf_own, wp_own = (item.astype(F32) for item in (w_out, w_fc, w_proj))
+    wo_own = w_out.astype(F32)
     wo_other = cross(wo_own)
-    wf_other = cross(wf_own)
-    wp_other = cross(wp_own)
-
-    def qkv_bias(flat):
-        return jnp.stack([flat[:width], jnp.zeros((width,), F32), flat[width : 2 * width]])
 
     own, other_front = front(
-        mine, tokens, segments.reshape(2, BIN), lengths,
-        ln1_gain.reshape(1, -1), ln1_bias.reshape(1, -1), w3, qkv_bias(small), width,
+        mine, tokens, segments.reshape(2, BIN), lengths, pack, w3, width,
     )
     qkv_own, attn_own, lse_own, h1, start, row = own
-    small_other, w3_other, h1 = lax.optimization_barrier((small_other, w3_other, h1))
-    qkv_other, attn_other, lse_other = other_front(h1, start, w3_other, qkv_bias(small_other))
-    vec_in = jnp.stack([out_bias, ln2_gain, ln2_bias, proj_bias]).astype(F32)
-    bfc = jnp.concatenate([small[2 * width :], small_other[2 * width :]]).reshape(-1, CHUNK)
+    pack_other, w3_other, h1 = lax.optimization_barrier((pack_other, w3_other, h1))
+    qkv_other, attn_other, lse_other = other_front(h1, start, pack_other, w3_other)
     arrays = (
         qkv_own, qkv_other, attn_own, attn_other, h1, w3, w3_other, tokens, cotangent,
-        wo_own, wo_other, wf_own, wf_other, wp_own, wp_other, lse_own, lse_other,
+        wo_own, wo_other, w_fc, w_proj, lse_own, lse_other,
     )
-    grad_proj, grad_fc, grad_out, grad_qkv, input_grad, block_sum, rows = back(
-        bits, arrays, row, ln1_gain.reshape(1, -1), vec_in, bfc, (pairs, hidden, model)
+    grad_proj, grad_fc, grad_out, grad_qkv, input_grad, block_out, _, rows = back(
+        bits, arrays, row, (pack, pack_other), (pairs, hidden, model)
     )
-    block_out = (block_sum + vec_in[3]).astype(BF16)
     grad_qkv = jnp.transpose(grad_qkv, (1, 0, 2))
     return (
         block_out,

time: 310 us -> 303 us (0.977)
  other arithmetic: 16.4 us -> 3.63 us
  local copies, waits for them, and re-layouts: 21.2 us -> 25.8 us
    convert_element_type x6 -> x1, other arithmetic: 12.4 us -> 0.08 us  [on_device(): wo_own = w_out.astype(F32)]
    unnamed x49 -> x55, local copies, waits for them, and re-layouts: 15 us -> 21.4 us
  transfers between devices with their start and end apart: 5 -> 3, of which waited for: 0 -> 0; matrix products, arithmetic and copies ran while one was open for 3% -> 1% of each run, Pallas kernels for 13% -> 13%
where the time goes in v1:
time: 303 us; the launch traced here: 302 us
  Pallas kernels  271 us (89%)
  local copies, waits for them, and re-layouts  25.8 us (9%)
  other arithmetic  3.63 us (1%)
    pallas_call x1, Pallas kernels, back(): pl.pallas_call(functools.partial(back_kernel, bits, groups), out_shape=[j...  232 us
    unnamed x55, local copies, waits for them, and re-layouts  21.4 us
    pallas_call x1, Pallas kernels, front(): return (own(mine, x, seg, lens, pack, w_own), other)  20.3 us
    pallas_call x1, Pallas kernels, other(): pl.pallas_call(other_front_kernel, out_shape=out_shapes, grid=(pairs,), i...  18.7 us
  transfers between devices with their start and end apart: 3, of which 0 were waited for; matrix products, arithmetic and copies ran while one was open for 1% of the time, Pallas kernels for 13%

profile of v1, /device:TPU:0, one launch (start us, length us, event | category | flops | bytes accessed | tf_op | source)
XLA Modules:
  0.0 302.2 jit_solution(1651887224938574516)
XLA Ops:
  0.6 0.0 copy-start.5
  0.7 0.0 copy-start.16
  0.7 0.0 copy-start.10
  0.7 0.0 copy-start.11
  0.7 0.0 copy-start.12
  0.7 0.0 copy-start.13
  0.7 0.0 copy-start.14
  0.7 0.0 copy-start.15
  0.7 3.5 %convert_bitcast_fusion.w_ref.w3_own_ref = f32[3,768,384]{2,1,0:T(8,128)} fusion(bf16[768,3,384]{2,0,1:T(8,128)(2,1)} %param.21), kind=kLoop, calls=%fused_computation | loop fusion | flops 884736 | bytes 5308416 | tf_op jit(solution)/shard_map/convert_element_type | solution.py:894
  4.3 0.5 collective-permute-start.1
  4.8 0.1 convert_element_type.22.wo_own_ref
  4.9 0.0 copy-start.1
  4.9 0.1 collective-permute-start.2
  5.0 0.0 copy-done.10
  5.0 0.2 dynamic-update-slice
  5.3 0.2 dynamic-update-slice.1
  5.5 0.2 dynamic-update-slice.2
  5.7 0.2 dynamic-update-slice.3
  5.9 0.2 dynamic-update-slice.4
  6.1 0.2 dynamic-update-slice.5
  6.3 0.2 dynamic-update-slice.6
  6.5 0.2 dynamic-update-slice.7
  6.8 0.5 collective-permute-start
  7.4 0.6 reshape.46.seg_ref
  8.0 20.3 %own_front.1 = (bf16[3,3,1024,128]{3,2,1,0:T(8,128)(2,1)}, bf16[3,1024,128]{2,1,0:T(8,128)(2,1)}, f32[3,8,1024]{2,1,0:T(8,128)}, bf16[1024,768]{1,0:T(8,128)(2,1...) custom-call(s32[1]{0:T(128)} %bitcast.mp_ref, bf16[2048,768]{1,0:T(8,128)(2,1)} %x_ref.3, s32[2,1024]{1,0:T(2,128)} %reshape.46.seg_ref, ...), custom_call_target="tpu_custom_call" | custom-call | flops 6000000000 | bytes 10000000 | tf_op jit(solution)/shard_map/own_front/pallas_call | solution.py:205
  28.3 0.0 collective-permute-done.pack_ref.pack_other_ref
  28.3 0.0 collective-permute-done.1.w_ref.w3_other_ref
  28.3 0.6 copy-done.7
  28.9 18.7 %other_front.1 = (bf16[3,3,1024,128]{3,2,1,0:T(8,128)(2,1)}, bf16[3,1024,128]{2,1,0:T(8,128)(2,1)}, f32[3,8,1024]{2,1,0:T(8,128)}) custom-call(bf16[1024,768]{1,0:T(8,128)(2,1)} %get-tuple-element.35.h1_ref, s32[1024,1]{1,0:T(8,128)} %get-tuple-element.36.start_ref, f32[9,768]{1,0:T(8,128)} %copy-done.7, f32[3,768,384]{2,1,0:T(8,128)} %collective-permute-done.1.w_ref.w3_other_ref), custom_call_target="tpu_custom_call" | custom-call | flops 6000000000 | bytes 10000000 | tf_op jit(solution)/shard_map/other_front/pallas_call | solution.py:194
  47.6 0.0 collective-permute-done.2.wo_other_ref
  47.6 1.0 copy-done.3
  48.6 231.8 %back.1 = (f32[1536,768]{1,0:T(8,128)}, f32[768,1536]{1,0:T(8,128)}, f32[384,768]{1,0:T(8,128)}, f32[3,768,384]{2,1,0:T(8,128)}, f32[2048,768]{1,0:T(8,128)}, /*...) custom-call(bf16[3,3,1024,128]{3,2,1,0:T(8,128)(2,1)} %get-tuple-element.33.qkv_own_ref, ...), custom_call_target="tpu_custom_call" | custom-call | tf_op jit(solution)/shard_map/back/pallas_call | solution.py:812
  280.4 0.7 slice.30
  281.1 1.6 slice_reduce_fusion
  282.8 0.6 reshape.49
  283.4 0.6 reshape_squeeze.3
  283.9 3.9 %copy.44 = bf16[2048,768]{1,0:T(8,128)(2,1)} copy(bf16[2048,768]{1,0:T(8,128)(2,1)} %get-tuple-element.73) | data formatting | bytes 6291456
  287.9 1.0 copy-done
  288.8 3.2 %copy.45 = f32[2048,768]{1,0:T(8,128)} copy(f32[2048,768]{1,0:T(8,128)S(1)} %copy-done) | data formatting | bytes 12582912
  292.0 1.3 copy-done.2
  293.3 1.8 copy.46
  295.1 0.3 copy-done.4
  295.4 1.0 copy.47
  296.4 0.0 slice-done.3
  296.4 2.4 copy.48
  298.8 0.8 slice-done
  299.6 0.3 slice-done.1
  300.0 2.2 copy.49
  (29 shorter events, 0.1 us)
Async XLA Ops:
  0.6 4.1 %copy-start.5 = (bf16[384,768]{1,0:T(8,128)(2,1)S(1)}, bf16[384,768]{1,0:T(8,128)(2,1)}, u32[]{:S(2)}) copy-start(bf16[384,768]{1,0:T(8,128)(2,1)} %param.23) | copy-start | bytes 1769476
  0.7 4.3 %copy-start.16 = (bf16[2,384]{1,0:T(2,128)(2,1)S(1)}, bf16[2,384]{1,0:T(2,128)(2,1)}, u32[]{:S(2)}) copy-start(bf16[2,384]{1,0:T(2,128)(2,1)} %param.22) | copy-start | bytes 4612
  0.7 4.3 %copy-start.10 = (bf16[768]{0:T(1024)(128)(2,1)S(1)}, bf16[768]{0:T(1024)(128)(2,1)}, u32[]{:S(2)}) copy-start(bf16[768]{0:T(1024)(128)(2,1)} %param.19) | copy-start | bytes 4612
  0.7 4.6 %copy-start.11 = (bf16[768]{0:T(1024)(128)(2,1)S(1)}, bf16[768]{0:T(1024)(128)(2,1)}, u32[]{:S(2)}) copy-start(bf16[768]{0:T(1024)(128)(2,1)} %param.20) | copy-start | bytes 4612
  0.7 4.8 %copy-start.12 = (bf16[768]{0:T(1024)(128)(2,1)S(1)}, bf16[768]{0:T(1024)(128)(2,1)}, u32[]{:S(2)}) copy-start(bf16[768]{0:T(1024)(128)(2,1)} %param.24) | copy-start | bytes 4612
  0.7 5.0 %copy-start.13 = (bf16[768]{0:T(1024)(128)(2,1)S(1)}, bf16[768]{0:T(1024)(128)(2,1)}, u32[]{:S(2)}) copy-start(bf16[768]{0:T(1024)(128)(2,1)} %param.25) | copy-start | bytes 4612
  0.7 5.2 %copy-start.14 = (bf16[768]{0:T(1024)(128)(2,1)S(1)}, bf16[768]{0:T(1024)(128)(2,1)}, u32[]{:S(2)}) copy-start(bf16[768]{0:T(1024)(128)(2,1)} %param.26) | copy-start | bytes 4612
  0.7 5.4 %copy-start.15 = (bf16[768]{0:T(1024)(128)(2,1)S(1)}, bf16[768]{0:T(1024)(128)(2,1)}, u32[]{:S(2)}) copy-start(bf16[768]{0:T(1024)(128)(2,1)} %param.30) | copy-start | bytes 4612
  0.7 5.8 %copy-start.9 = (bf16[1536]{0:T(1024)(128)(2,1)S(1)}, bf16[1536]{0:T(1024)(128)(2,1)}, u32[]{:S(2)}) copy-start(bf16[1536]{0:T(1024)(128)(2,1)} %param.28) | copy-start | bytes 9220
  0.7 6.6 %copy-start.8 = (s32[2048]{0:T(1024)S(1)}, s32[2048]{0:T(1024)}, u32[]{:S(2)}) copy-start(s32[2048]{0:T(1024)} %param.17) | copy-start | bytes 24580
  4.3 24.0 %collective-permute-start.1 = (f32[3,768,384]{2,1,0:T(8,128)}, f32[3,768,384]{2,1,0:T(8,128)}, u32[]{:S(2)}, u32[]{:S(2)}) collective-permute-start(f32[3,768,384]{2,1,0:T(8,128)} %convert_bitcast_fusion.w_ref.w3_own_ref), channel_id=1, source_target_pairs={{0,1},{1,0},{2,3},{3,2},{4,5},{5,4},{6,7},{7,6},{8,9},{9,8},{10,11... | collective-permute-start | bytes 10616840 | tf_op jit(solution)/shard_map/ppermute | solution.py:892
  4.9 23.4 %copy-start.1 = (f32[384,768]{1,0:T(8,128)}, f32[384,768]{1,0:T(8,128)S(1)}, u32[]{:S(2)}) copy-start(f32[384,768]{1,0:T(8,128)S(1)} %convert_element_type.22.wo_own_ref) | copy-start | bytes 3538948
  4.9 42.7 %collective-permute-start.2 = (f32[384,768]{1,0:T(8,128)S(1)}, f32[384,768]{1,0:T(8,128)S(1)}, u32[]{:S(2)}, u32[]{:S(2)}) collective-permute-start(f32[384,768]{1,0:T(8,128)S(1)} %convert_element_type.22.wo_own_ref), channel_id=1, source_target_pairs={{0,1},{1,0},{2,3},{3,2},{4,5},{5,4},{6,7},{7,6},{8,9},{9,8},{10,11... | collective-permute-start | bytes 3538952 | tf_op jit(solution)/shard_map/ppermute | solution.py:892
  6.8 1.2 copy-start.6
  6.8 21.5 %collective-permute-start = (f32[9,768]{1,0:T(8,128)S(1)}, f32[9,768]{1,0:T(8,128)S(1)}, u32[]{:S(2)}, u32[]{:S(2)}) collective-permute-start(f32[9,768]{1,0:T(8,128)S(1)} %reshape.51.pack_ref), channel_id=1, source_target_pairs={{0,1},{1,0},{2,3},{3,2},{4,5},{5,4},{6,7},{7,6},{8,9},{9,8},{10,11... | collective-permute-start | bytes 82952 | tf_op jit(solution)/shard_map/ppermute | solution.py:892
  28.3 0.6 copy-start.7
  47.6 1.0 copy-start.3
  283.9 4.9 %copy-start = (f32[2048,768]{1,0:T(8,128)S(1)}, f32[2048,768]{1,0:T(8,128)}, u32[]{:S(2)}) copy-start(f32[2048,768]{1,0:T(8,128)} %get-tuple-element.74) | copy-start | bytes 18874372
  283.9 12.5 %slice-start.2 = ((s8[4718592]{0:T(1024)(128)(4,1)}), s8[4194304]{0:T(1024)(128)(4,1)S(1)}, s32[]{:S(2)}) async-start(s8[4718592]{0:T(1024)(128)(4,1)} %bitcast.6), calls=%async_computation.2 | async-start | bytes 8388608
  288.8 4.5 %copy-start.2 = (f32[3,768,384]{2,1,0:T(8,128)S(1)}, f32[3,768,384]{2,1,0:T(8,128)}, u32[]{:S(2)}) copy-start(f32[3,768,384]{2,1,0:T(8,128)} %get-tuple-element.48) | copy-start | bytes 10616836
  288.8 7.6 %slice-start.3 = ((s8[4718592]{0:T(1024)(128)(4,1)}), s8[524288]{0:T(1024)(128)(4,1)S(1)}, s32[]{:S(2)}) async-start(s8[4718592]{0:T(1024)(128)(4,1)} %bitcast.6), calls=%async_computation.3 | async-start | bytes 1048576
  293.3 2.1 copy-start.4
  295.4 4.2 %slice-start = ((s8[4718592]{0:T(1024)(128)(4,1)}), s8[4194304]{0:T(1024)(128)(4,1)S(1)}, s32[]{:S(2)}) async-start(s8[4718592]{0:T(1024)(128)(4,1)} %bitcast.4), calls=%async_computation | async-start | bytes 8388608
  296.4 3.5 %slice-start.1 = ((s8[4718592]{0:T(1024)(128)(4,1)}), s8[524288]{0:T(1024)(128)(4,1)S(1)}, s32[]{:S(2)}) async-start(s8[4718592]{0:T(1024)(128)(4,1)} %bitcast.4), calls=%async_computation.1 | async-start | bytes 1048576

commit v2 on v1

--- a/solution.py
+++ b/solution.py
@@ -85,23 +85,26 @@
         j = lax.broadcasted_iota(jnp.int32, (BLOCK, seen), 1)
         i = lax.broadcasted_iota(jnp.int32, (BLOCK, seen), 0) + block * BLOCK
         visible = (j >= start_ref[rows]) & (j <= i)
-        mixed = []
+        both = jnp.concatenate([queries * head_mask(head, score_scale) for head in range(2)], axis=0)
+        scores = dot_nt(both, key_rows).reshape(2, BLOCK, seen)
+        scores = jnp.where(visible[None], scores, masked_score)
+        highest = jnp.max(scores, axis=-1, keepdims=True)
+        weights = jnp.exp(scores - highest)
+        totals = jnp.sum(weights, axis=-1, keepdims=True)
+        mixed = dot_nn(weights.astype(BF16).reshape(2 * BLOCK, seen), value_rows).reshape(2, BLOCK, PAIR) / totals
+        logs = highest + jnp.log(totals)
         for head in range(2):
-            scores = dot_nt(queries * head_mask(head, score_scale), key_rows)
-            scores = jnp.where(visible, scores, masked_score)
-            highest = jnp.max(scores, axis=-1, keepdims=True)
-            weights = jnp.exp(scores - highest)
-            totals = jnp.sum(weights, axis=-1, keepdims=True)
-            mixed.append(dot_nn(weights.astype(BF16), value_rows) / totals)
-            lse_ref[0, head : head + 1, rows] = column_to_row(highest + jnp.log(totals))
+            lse_ref[0, head : head + 1, rows] = column_to_row(logs[head])
         attn_ref[0, rows] = jnp.where(lane < HEAD_DIM, mixed[0], mixed[1]).astype(BF16)
 
 
 def project_and_attend(h1, w_ref, pack_ref, start_ref, qkv_ref, attn_ref, lse_ref):
     width = pl.num_programs(0) * PAIR
     place = pl.program_id(0) * PAIR
+    weights = jnp.concatenate([w_ref[c].astype(BF16) for c in range(3)], axis=1)
+    projected = dot_nn(h1, weights)
     for c in range(3):
-        out = dot_nn(h1, w_ref[c].astype(BF16))
+        out = projected[:, c * PAIR : (c + 1) * PAIR]
         if c != 1:
             at = place if c == 0 else width + place
             out = out + pack_ref[QV_ROW : QV_ROW + 1, pl.ds(pl.multiple_of(at, PAIR), PAIR)]
@@ -316,7 +319,7 @@
     load(lse_other_ref, lse.at[pairs : 2 * pairs])
 
     def block_loads(b):
-        slot = b % 2
+        slot = b % 3
         at = pl.ds(pl.multiple_of(b * CHUNK, CHUNK), CHUNK)
         return [
             pltpu.make_async_copy(wf_ref.at[:, at], wf_low.at[slot], bsem.at[slot, 0]),
@@ -336,13 +339,13 @@
     def send_block(b):
         for item in block_loads(b):
             item.wait()
-        wf_out[...] = wf_low[b % 2].astype(F32)
-        wp_out[...] = wp_low[b % 2].astype(F32)
+        wf_out[...] = wf_low[b % 3].astype(F32)
+        wp_out[...] = wp_low[b % 3].astype(F32)
         for item in block_sends(b):
             item.start()
 
     def w3_loads(q, begin):
-        slot = q % 2
+        slot = 1 - q % 2
         at = pl.ds(pl.multiple_of((q // 2) * PAIR, PAIR), PAIR)
         for half, ref in ((0, w3_own_ref), (1, w3_other_ref)):
             @pl.when(slot == half)
@@ -480,22 +483,22 @@
     attend_tick = middle_tick + 1
     input_tick = attend_tick + 2 * pairs
     late = chunks - 4
-    late_tick = late + 4
-    arrivals = [(middle_tick + 2, [0]), (middle_tick + 4, [1, 2]), (middle_tick + 6, [3]), (middle_tick + 8, [4, 5])]
-    ticks = chunks + 4 + offsets[stages] + 1
+    late_tick = late + 3
+    arrivals = [(middle_tick + 2, [0]), (middle_tick + 3, [1, 2]), (middle_tick + 5, [3]), (middle_tick + 7, [4, 5])]
+    ticks = chunks + 3 + offsets[stages] + 1
 
     def at_stage(t, shift):
         since = t - shift
-        early = (since >= 3) & (since < late + 3)
-        last = (since >= late_tick) & (since < chunks + 4)
-        c = jnp.where(since < late_tick, since - 3, since - late_tick + late)
+        early = (since >= 2) & (since < late + 2)
+        last = (since >= late_tick) & (since < chunks + 3)
+        c = jnp.where(since < late_tick, since - 2, since - late_tick + late)
         return jnp.clip(c, 0, chunks - 1), early | last
 
     def ring_tick(t):
-        @pl.when((t >= 3) & (t % 2 == 1) & (t < middle_tick + 3))
-        def _():
-            mp_finish(t - 3)
+        @pl.when((t >= 2) & (t % 2 == 0) & (t < middle_tick + 2))
+        def _():
             mp_finish(t - 2)
+            mp_finish(t - 1)
 
         for at, made in arrivals:
             @pl.when(t == at)
@@ -552,7 +555,7 @@
         loads[early].wait()
 
     def hidden_half(u):
-        b, half = u // 2, u % 2
+        b, half = u // 2, 1 - u % 2
 
         @pl.when(half == 1)
         def _():
@@ -568,11 +571,11 @@
                 for item in block_loads(b + 2):
                     item.start()
 
-            wf_low[2] = wf[b % 2].astype(BF16)
-            wp_low[2] = wp[b % 2].astype(BF16)
+            wf_low[3] = wf[b % 2].astype(BF16)
+            wp_low[3] = wp[b % 2].astype(BF16)
 
         span = 2 * BLOCK
-        place = jnp.where(half == 0, b % 2, 2)
+        place = jnp.where(half == 0, b % 3, 3)
         fc = wf_low[place]
         proj = wp_low[place]
         at = pl.ds(FC_ROW + b // pieces, 1), pl.ds(pl.multiple_of((b % pieces) * CHUNK, CHUNK), CHUNK)
@@ -669,7 +672,7 @@
             item.wait()
 
     def attend_half(q):
-        p, half = q // 2, q % 2
+        p, half = q // 2, 1 - q % 2
 
         @pl.when(q + 1 < 2 * pairs)
         def _():
@@ -689,7 +692,7 @@
             put_piece(half, pairs * (p + 1) + n % pairs, n // pairs, grad[n * PAIR : (n + 1) * PAIR])
         weights = jnp.concatenate([w3[half, c].astype(BF16) for c in range(3)], axis=1)
         dwide[...] = dwide[...] + dot_nt(low, weights)
-        for at, made in ((1, [1, 2]), (3, [3]), (5, [4, 5])):
+        for at, made in ((0, [1, 2]), (2, [3]), (4, [4, 5])):
             @pl.when(q == at)
             def _():
                 for n in made:
@@ -839,8 +842,8 @@
             pltpu.VMEM((BIN, model), F32),
             pltpu.VMEM((2, model, CHUNK), F32),
             pltpu.VMEM((2, CHUNK, model), F32),
-            pltpu.VMEM((3, model, CHUNK), BF16),
-            pltpu.VMEM((3, CHUNK, model), BF16),
+            pltpu.VMEM((4, model, CHUNK), BF16),
+            pltpu.VMEM((4, CHUNK, model), BF16),
             pltpu.VMEM((model, CHUNK), F32),
             pltpu.VMEM((CHUNK, model), F32),
             pltpu.VMEM((2, width, model), F32),
@@ -858,7 +861,7 @@
             dma((LANDS,)),
             dma((SLOTS, 12)),
             dma((10,)),
-            dma((2, 2)),
+            dma((3, 2)),
             dma((2,)),
             dma((2, 2)),
             dma((2, 3)),

time: 303 us -> 291 us (0.960)
  Pallas kernels: 271 us -> 260 us
    pallas_call x1, Pallas kernels: 18.7 us -> 14.6 us  [other(): pl.pallas_call(other_front_kernel, out_shape=out_shapes, grid=(pairs,), i...]
    pallas_call x1, Pallas kernels: 20.3 us -> 16.7 us  [front(): return (own(mine, x, seg, lens, pack, w_own), other)]
    pallas_call x1, Pallas kernels: 232 us -> 228 us  [back(): pl.pallas_call(functools.partial(back_kernel, bits, groups), out_shape=[j...]
  transfers between devices with their start and end apart: 3 -> 3, of which waited for: 0 -> 0; matrix products, arithmetic and copies ran while one was open for 1% -> 1% of each run, Pallas kernels for 13% -> 11%
where the time goes in v2:
time: 291 us
  Pallas kernels  260 us (89%)
  local copies, waits for them, and re-layouts  25.8 us (9%)
  other arithmetic  3.63 us (1%)
    pallas_call x1, Pallas kernels, back(): pl.pallas_call(functools.partial(back_kernel, bits, groups), out_shape=[j...  228 us
    unnamed x55, local copies, waits for them, and re-layouts  21.4 us
    pallas_call x1, Pallas kernels, front(): return (own(mine, x, seg, lens, pack, w_own), other)  16.7 us
    pallas_call x1, Pallas kernels, other(): pl.pallas_call(other_front_kernel, out_shape=out_shapes, grid=(pairs,), i...  14.6 us
  transfers between devices with their start and end apart: 3, of which 0 were waited for; matrix products, arithmetic and copies ran while one was open for 1% of the time, Pallas kernels for 11%

profile of v2, /device:TPU:0, one launch (start us, length us, event | category | flops | bytes accessed | tf_op | source)
XLA Modules:
  0.0 291.0 jit_solution(13226644823240447363)
XLA Ops:
  0.6 0.0 copy-start.5
  0.7 0.0 copy-start.16
  0.7 0.0 copy-start.10
  0.7 0.0 copy-start.11
  0.7 0.0 copy-start.12
  0.7 0.0 copy-start.13
  0.7 0.0 copy-start.14
  0.7 0.0 copy-start.15
  0.7 0.0 copy-start.9
  0.7 0.0 copy-start.8
  0.7 3.5 %convert_bitcast_fusion.w_ref.w3_own_ref = f32[3,768,384]{2,1,0:T(8,128)} fusion(bf16[768,3,384]{2,0,1:T(8,128)(2,1)} %param.21), kind=kLoop, calls=%fused_computation | loop fusion | flops 884736 | bytes 5308416 | tf_op jit(solution)/shard_map/convert_element_type | solution.py:897
  4.3 0.5 collective-permute-start.1
  4.8 0.1 convert_element_type.22.wo_own_ref
  4.9 0.0 copy-start.1
  4.9 0.1 collective-permute-start.2
  5.0 0.2 dynamic-update-slice
  5.3 0.2 dynamic-update-slice.1
  5.5 0.2 dynamic-update-slice.2
  5.7 0.2 dynamic-update-slice.3
  5.9 0.2 dynamic-update-slice.4
  6.1 0.2 dynamic-update-slice.5
  6.3 0.2 dynamic-update-slice.6
  6.5 0.2 dynamic-update-slice.7
  6.8 0.5 collective-permute-start
  7.4 0.6 reshape.46.seg_ref
  8.0 16.7 %own_front.1 = (bf16[3,3,1024,128]{3,2,1,0:T(8,128)(2,1)}, bf16[3,1024,128]{2,1,0:T(8,128)(2,1)}, f32[3,8,1024]{2,1,0:T(8,128)}, bf16[1024,768]{1,0:T(8,128)(2,1...) custom-call(s32[1]{0:T(128)} %bitcast.mp_ref, bf16[2048,768]{1,0:T(8,128)(2,1)} %x_ref.3, s32[2,1024]{1,0:T(2,128)} %reshape.46.seg_ref, ...), custom_call_target="tpu_custom_call" | custom-call | flops 6000000000 | bytes 10000000 | tf_op jit(solution)/shard_map/own_front/pallas_call | solution.py:208
  24.7 0.0 collective-permute-done.pack_ref.pack_other_ref
  24.7 0.0 collective-permute-done.1.w_ref.w3_other_ref
  24.7 0.6 copy-done.7
  25.3 14.6 %other_front.1 = (bf16[3,3,1024,128]{3,2,1,0:T(8,128)(2,1)}, bf16[3,1024,128]{2,1,0:T(8,128)(2,1)}, f32[3,8,1024]{2,1,0:T(8,128)}) custom-call(bf16[1024,768]{1,0:T(8,128)(2,1)} %get-tuple-element.35.h1_ref, s32[1024,1]{1,0:T(8,128)} %get-tuple-element.36.start_ref, f32[9,768]{1,0:T(8,128)} %copy-done.7, f32[3,768,384]{2,1,0:T(8,128)} %collective-permute-done.1.w_ref.w3_other_ref), custom_call_target="tpu_custom_call" | custom-call | flops 6000000000 | bytes 10000000 | tf_op jit(solution)/shard_map/other_front/pallas_call | solution.py:197
  39.9 0.0 collective-permute-done.2.wo_other_ref
  39.9 1.0 copy-done.3
  40.9 228.3 %back.1 = (f32[1536,768]{1,0:T(8,128)}, f32[768,1536]{1,0:T(8,128)}, f32[384,768]{1,0:T(8,128)}, f32[3,768,384]{2,1,0:T(8,128)}, f32[2048,768]{1,0:T(8,128)}, /*...) custom-call(bf16[3,3,1024,128]{3,2,1,0:T(8,128)(2,1)} %get-tuple-element.33.qkv_own_ref, ...), custom_call_target="tpu_custom_call" | custom-call | tf_op jit(solution)/shard_map/back/pallas_call | solution.py:815
  269.2 0.7 slice.30
  269.9 1.6 slice_reduce_fusion
  271.6 0.6 reshape.49
  272.2 0.6 reshape_squeeze.3
  272.8 3.9 %copy.44 = bf16[2048,768]{1,0:T(8,128)(2,1)} copy(bf16[2048,768]{1,0:T(8,128)(2,1)} %get-tuple-element.73) | data formatting | bytes 6291456
  276.7 1.0 copy-done
  277.6 3.2 %copy.45 = f32[2048,768]{1,0:T(8,128)} copy(f32[2048,768]{1,0:T(8,128)S(1)} %copy-done) | data formatting | bytes 12582912
  280.8 1.3 copy-done.2
  282.1 1.8 copy.46
  283.9 0.3 copy-done.4
  284.2 1.0 copy.47
  285.3 2.4 copy.48
  287.7 0.8 slice-done
  288.5 0.3 slice-done.1
  288.8 2.2 copy.49
  (29 shorter events, 0.1 us)
Async XLA Ops:
  0.6 4.1 %copy-start.5 = (bf16[384,768]{1,0:T(8,128)(2,1)S(1)}, bf16[384,768]{1,0:T(8,128)(2,1)}, u32[]{:S(2)}) copy-start(bf16[384,768]{1,0:T(8,128)(2,1)} %param.23) | copy-start | bytes 1769476
  0.7 4.3 %copy-start.16 = (bf16[2,384]{1,0:T(2,128)(2,1)S(1)}, bf16[2,384]{1,0:T(2,128)(2,1)}, u32[]{:S(2)}) copy-start(bf16[2,384]{1,0:T(2,128)(2,1)} %param.22) | copy-start | bytes 4612
  0.7 4.3 %copy-start.10 = (bf16[768]{0:T(1024)(128)(2,1)S(1)}, bf16[768]{0:T(1024)(128)(2,1)}, u32[]{:S(2)}) copy-start(bf16[768]{0:T(1024)(128)(2,1)} %param.19) | copy-start | bytes 4612
  0.7 4.6 %copy-start.11 = (bf16[768]{0:T(1024)(128)(2,1)S(1)}, bf16[768]{0:T(1024)(128)(2,1)}, u32[]{:S(2)}) copy-start(bf16[768]{0:T(1024)(128)(2,1)} %param.20) | copy-start | bytes 4612
  0.7 4.8 %copy-start.12 = (bf16[768]{0:T(1024)(128)(2,1)S(1)}, bf16[768]{0:T(1024)(128)(2,1)}, u32[]{:S(2)}) copy-start(bf16[768]{0:T(1024)(128)(2,1)} %param.24) | copy-start | bytes 4612
  0.7 5.0 %copy-start.13 = (bf16[768]{0:T(1024)(128)(2,1)S(1)}, bf16[768]{0:T(1024)(128)(2,1)}, u32[]{:S(2)}) copy-start(bf16[768]{0:T(1024)(128)(2,1)} %param.25) | copy-start | bytes 4612
  0.7 5.2 %copy-start.14 = (bf16[768]{0:T(1024)(128)(2,1)S(1)}, bf16[768]{0:T(1024)(128)(2,1)}, u32[]{:S(2)}) copy-start(bf16[768]{0:T(1024)(128)(2,1)} %param.26) | copy-start | bytes 4612
  0.7 5.4 %copy-start.15 = (bf16[768]{0:T(1024)(128)(2,1)S(1)}, bf16[768]{0:T(1024)(128)(2,1)}, u32[]{:S(2)}) copy-start(bf16[768]{0:T(1024)(128)(2,1)} %param.30) | copy-start | bytes 4612
  0.7 5.8 %copy-start.9 = (bf16[1536]{0:T(1024)(128)(2,1)S(1)}, bf16[1536]{0:T(1024)(128)(2,1)}, u32[]{:S(2)}) copy-start(bf16[1536]{0:T(1024)(128)(2,1)} %param.28) | copy-start | bytes 9220
  0.7 6.6 %copy-start.8 = (s32[2048]{0:T(1024)S(1)}, s32[2048]{0:T(1024)}, u32[]{:S(2)}) copy-start(s32[2048]{0:T(1024)} %param.17) | copy-start | bytes 24580
  4.3 20.4 %collective-permute-start.1 = (f32[3,768,384]{2,1,0:T(8,128)}, f32[3,768,384]{2,1,0:T(8,128)}, u32[]{:S(2)}, u32[]{:S(2)}) collective-permute-start(f32[3,768,384]{2,1,0:T(8,128)} %convert_bitcast_fusion.w_ref.w3_own_ref), channel_id=1, source_target_pairs={{0,1},{1,0},{2,3},{3,2},{4,5},{5,4},{6,7},{7,6},{8,9},{9,8},{10,11... | collective-permute-start | bytes 10616840 | tf_op jit(solution)/shard_map/ppermute | solution.py:895
  4.9 19.8 %copy-start.1 = (f32[384,768]{1,0:T(8,128)}, f32[384,768]{1,0:T(8,128)S(1)}, u32[]{:S(2)}) copy-start(f32[384,768]{1,0:T(8,128)S(1)} %convert_element_type.22.wo_own_ref) | copy-start | bytes 3538948
  4.9 35.0 %collective-permute-start.2 = (f32[384,768]{1,0:T(8,128)S(1)}, f32[384,768]{1,0:T(8,128)S(1)}, u32[]{:S(2)}, u32[]{:S(2)}) collective-permute-start(f32[384,768]{1,0:T(8,128)S(1)} %convert_element_type.22.wo_own_ref), channel_id=1, source_target_pairs={{0,1},{1,0},{2,3},{3,2},{4,5},{5,4},{6,7},{7,6},{8,9},{9,8},{10,11... | collective-permute-start | bytes 3538952 | tf_op jit(solution)/shard_map/ppermute | solution.py:895
  6.8 1.2 copy-start.6
  6.8 17.9 %collective-permute-start = (f32[9,768]{1,0:T(8,128)S(1)}, f32[9,768]{1,0:T(8,128)S(1)}, u32[]{:S(2)}, u32[]{:S(2)}) collective-permute-start(f32[9,768]{1,0:T(8,128)S(1)} %reshape.51.pack_ref), channel_id=1, source_target_pairs={{0,1},{1,0},{2,3},{3,2},{4,5},{5,4},{6,7},{7,6},{8,9},{9,8},{10,11... | collective-permute-start | bytes 82952 | tf_op jit(solution)/shard_map/ppermute | solution.py:895
  24.7 0.6 copy-start.7
  39.9 1.0 copy-start.3
  272.8 4.9 %copy-start = (f32[2048,768]{1,0:T(8,128)S(1)}, f32[2048,768]{1,0:T(8,128)}, u32[]{:S(2)}) copy-start(f32[2048,768]{1,0:T(8,128)} %get-tuple-element.74) | copy-start | bytes 18874372
  272.8 12.5 %slice-start.2 = ((s8[4718592]{0:T(1024)(128)(4,1)}), s8[4194304]{0:T(1024)(128)(4,1)S(1)}, s32[]{:S(2)}) async-start(s8[4718592]{0:T(1024)(128)(4,1)} %bitcast.6), calls=%async_computation.2 | async-start | bytes 8388608
  277.6 4.5 %copy-start.2 = (f32[3,768,384]{2,1,0:T(8,128)S(1)}, f32[3,768,384]{2,1,0:T(8,128)}, u32[]{:S(2)}) copy-start(f32[3,768,384]{2,1,0:T(8,128)} %get-tuple-element.48) | copy-start | bytes 10616836
  277.6 7.6 %slice-start.3 = ((s8[4718592]{0:T(1024)(128)(4,1)}), s8[524288]{0:T(1024)(128)(4,1)S(1)}, s32[]{:S(2)}) async-start(s8[4718592]{0:T(1024)(128)(4,1)} %bitcast.6), calls=%async_computation.3 | async-start | bytes 1048576
  282.1 2.1 copy-start.4
  284.2 4.2 %slice-start = ((s8[4718592]{0:T(1024)(128)(4,1)}), s8[4194304]{0:T(1024)(128)(4,1)S(1)}, s32[]{:S(2)}) async-start(s8[4718592]{0:T(1024)(128)(4,1)} %bitcast.4), calls=%async_computation | async-start | bytes 8388608
  285.3 3.5 %slice-start.1 = ((s8[4718592]{0:T(1024)(128)(4,1)}), s8[524288]{0:T(1024)(128)(4,1)S(1)}, s32[]{:S(2)}) async-start(s8[4718592]{0:T(1024)(128)(4,1)} %bitcast.4), calls=%async_computation.1 | async-start | bytes 1048576

commit v3 on v2

--- a/solution.py
+++ b/solution.py
@@ -76,22 +76,29 @@
 
 def attend_pair(qkv_ref, start_ref, attn_ref, lse_ref):
     lane = lax.broadcasted_iota(jnp.int32, (1, PAIR), 1)
-    for block in range(BIN // BLOCK):
+    blocks = BIN // BLOCK
+
+    def score(block):
+        queries = qkv_ref[0, 0, block * BLOCK : (block + 1) * BLOCK]
+        both = jnp.concatenate([queries * head_mask(head, score_scale) for head in range(2)], axis=0)
+        return dot_nt(both, qkv_ref[0, 1, 0 : (block + 1) * BLOCK])
+
+    ahead = score(0)
+    for block in range(blocks):
         rows = slice(block * BLOCK, (block + 1) * BLOCK)
         seen = (block + 1) * BLOCK
-        queries = qkv_ref[0, 0, rows]
-        key_rows = qkv_ref[0, 1, 0:seen]
-        value_rows = qkv_ref[0, 2, 0:seen]
+        scores = ahead.reshape(2, BLOCK, seen)
+        if block + 1 < blocks:
+            ahead = score(block + 1)
         j = lax.broadcasted_iota(jnp.int32, (BLOCK, seen), 1)
         i = lax.broadcasted_iota(jnp.int32, (BLOCK, seen), 0) + block * BLOCK
         visible = (j >= start_ref[rows]) & (j <= i)
-        both = jnp.concatenate([queries * head_mask(head, score_scale) for head in range(2)], axis=0)
-        scores = dot_nt(both, key_rows).reshape(2, BLOCK, seen)
         scores = jnp.where(visible[None], scores, masked_score)
         highest = jnp.max(scores, axis=-1, keepdims=True)
         weights = jnp.exp(scores - highest)
         totals = jnp.sum(weights, axis=-1, keepdims=True)
-        mixed = dot_nn(weights.astype(BF16).reshape(2 * BLOCK, seen), value_rows).reshape(2, BLOCK, PAIR) / totals
+        mixed = dot_nn(weights.astype(BF16).reshape(2 * BLOCK, seen), qkv_ref[0, 2, 0:seen])
+        mixed = mixed.reshape(2, BLOCK, PAIR) / totals
         logs = highest + jnp.log(totals)
         for head in range(2):
             lse_ref[0, head : head + 1, rows] = column_to_row(logs[head])
@@ -906,7 +913,7 @@
         mine, tokens, segments.reshape(2, BIN), lengths, pack, w3, width,
     )
     qkv_own, attn_own, lse_own, h1, start, row = own
-    pack_other, w3_other, h1 = lax.optimization_barrier((pack_other, w3_other, h1))
+    pack_other, w3_other, wo_other, h1 = lax.optimization_barrier((pack_other, w3_other, wo_other, h1))
     qkv_other, attn_other, lse_other = other_front(h1, start, pack_other, w3_other)
     arrays = (
         qkv_own, qkv_other, attn_own, attn_other, h1, w3, w3_other, tokens, cotangent,

time: 291 us -> 287 us (0.986)
  Pallas kernels: 260 us -> 256 us
  transfers between devices with their start and end apart: 3 -> 3, of which waited for: 0 -> 0; matrix products, arithmetic and copies ran while one was open for 1% -> 1% of each run, Pallas kernels for 11% -> 5%
where the time goes in v3:
time: 287 us; the launch traced here: 286 us
  Pallas kernels  256 us (89%)
  local copies, waits for them, and re-layouts  24.8 us (9%)
  other arithmetic  3.63 us (1%)
    pallas_call x1, Pallas kernels, back(): pl.pallas_call(functools.partial(back_kernel, bits, groups), out_shape=[j...  228 us
    unnamed x55, local copies, waits for them, and re-layouts  20.3 us
    pallas_call x1, Pallas kernels, front(): return (own(mine, x, seg, lens, pack, w_own), other)  14.7 us
    pallas_call x1, Pallas kernels, other(): pl.pallas_call(other_front_kernel, out_shape=out_shapes, grid=(pairs,), i...  12.9 us
  transfers between devices with their start and end apart: 3, of which 0 were waited for; matrix products, arithmetic and copies ran while one was open for 1% of the time, Pallas kernels for 5%

profile of v3, /device:TPU:0, one launch (start us, length us, event | category | flops | bytes accessed | tf_op | source)
XLA Modules:
  0.0 286.3 jit_solution(12453931545277125456)
XLA Ops:
  0.6 0.0 copy-start.5
  0.7 0.0 copy-start.16
  0.7 0.0 copy-start.10
  0.7 3.5 %convert_bitcast_fusion.w_ref.w3_own_ref = f32[3,768,384]{2,1,0:T(8,128)} fusion(bf16[768,3,384]{2,0,1:T(8,128)(2,1)} %param.21), kind=kLoop, calls=%fused_computation | loop fusion | flops 884736 | bytes 5308416 | tf_op jit(solution)/shard_map/convert_element_type | solution.py:904
  4.3 0.5 collective-permute-start.1
  4.8 0.0 copy-done.5
  4.8 0.1 convert_element_type.22.wo_own_ref
  4.9 0.0 copy-start.1
  4.9 0.1 collective-permute-start.2
  5.0 0.2 dynamic-update-slice
  5.3 0.0 copy-done.11
  5.3 0.2 dynamic-update-slice.1
  5.5 0.0 copy-done.12
  5.5 0.2 dynamic-update-slice.2
  5.7 0.2 dynamic-update-slice.3
  5.9 0.2 dynamic-update-slice.4
  6.1 0.2 dynamic-update-slice.5
  6.3 0.2 dynamic-update-slice.6
  6.5 0.0 copy-done.9
  6.5 0.2 dynamic-update-slice.7
  6.8 0.5 collective-permute-start
  7.4 0.6 reshape.46.seg_ref
  8.0 14.7 %own_front.1 = (bf16[3,3,1024,128]{3,2,1,0:T(8,128)(2,1)}, bf16[3,1024,128]{2,1,0:T(8,128)(2,1)}, f32[3,8,1024]{2,1,0:T(8,128)}, bf16[1024,768]{1,0:T(8,128)(2,1...) custom-call(s32[1]{0:T(128)} %bitcast.mp_ref, bf16[2048,768]{1,0:T(8,128)(2,1)} %x_ref.3, s32[2,1024]{1,0:T(2,128)} %reshape.46.seg_ref, ...), custom_call_target="tpu_custom_call" | custom-call | flops 6000000000 | bytes 10000000 | tf_op jit(solution)/shard_map/own_front/pallas_call | solution.py:215
  22.6 0.0 collective-permute-done.pack_ref.pack_other_ref
  22.6 0.0 copy-start.7
  22.6 0.0 collective-permute-done.2.wo_other_ref
  22.7 0.0 copy-start.3
  22.7 0.0 collective-permute-done.1.w_ref.w3_other_ref
  22.7 0.6 copy-done.7
  23.3 12.9 %other_front.1 = (bf16[3,3,1024,128]{3,2,1,0:T(8,128)(2,1)}, bf16[3,1024,128]{2,1,0:T(8,128)(2,1)}, f32[3,8,1024]{2,1,0:T(8,128)}) custom-call(bf16[1024,768]{1,0:T(8,128)(2,1)} %get-tuple-element.36.h1_ref, s32[1024,1]{1,0:T(8,128)} %get-tuple-element.37.start_ref, f32[9,768]{1,0:T(8,128)} %copy-done.7, f32[3,768,384]{2,1,0:T(8,128)} %collective-permute-done.1.w_ref.w3_other_ref), custom_call_target="tpu_custom_call" | custom-call | flops 6000000000 | bytes 10000000 | tf_op jit(solution)/shard_map/other_front/pallas_call | solution.py:204
  36.2 0.0 copy-done.3
  36.2 228.3 %back.1 = (f32[1536,768]{1,0:T(8,128)}, f32[768,1536]{1,0:T(8,128)}, f32[384,768]{1,0:T(8,128)}, f32[3,768,384]{2,1,0:T(8,128)}, f32[2048,768]{1,0:T(8,128)}, /*...) custom-call(bf16[3,3,1024,128]{3,2,1,0:T(8,128)(2,1)} %get-tuple-element.34.qkv_own_ref, ...), custom_call_target="tpu_custom_call" | custom-call | tf_op jit(solution)/shard_map/back/pallas_call | solution.py:822
  264.5 0.7 slice.30
  265.3 1.6 slice_reduce_fusion
  266.9 0.6 reshape.49
  267.5 0.6 reshape_squeeze.3
  268.1 3.9 %copy.44 = bf16[2048,768]{1,0:T(8,128)(2,1)} copy(bf16[2048,768]{1,0:T(8,128)(2,1)} %get-tuple-element.75) | data formatting | bytes 6291456
  272.0 1.0 copy-done
  273.0 3.2 %copy.45 = f32[2048,768]{1,0:T(8,128)} copy(f32[2048,768]{1,0:T(8,128)S(1)} %copy-done) | data formatting | bytes 12582912
  276.2 1.3 copy-done.2
  277.5 1.8 copy.46
  279.2 0.3 copy-done.4
  279.6 1.0 copy.47
  280.6 0.0 slice-done.3
  280.6 2.4 copy.48
  283.0 0.8 slice-done
  283.8 0.3 slice-done.1
  284.1 2.2 copy.49
  (29 shorter events, 0.1 us)
Async XLA Ops:
  0.6 4.1 %copy-start.5 = (bf16[384,768]{1,0:T(8,128)(2,1)S(1)}, bf16[384,768]{1,0:T(8,128)(2,1)}, u32[]{:S(2)}) copy-start(bf16[384,768]{1,0:T(8,128)(2,1)} %param.23) | copy-start | bytes 1769476
  0.7 4.3 %copy-start.16 = (bf16[2,384]{1,0:T(2,128)(2,1)S(1)}, bf16[2,384]{1,0:T(2,128)(2,1)}, u32[]{:S(2)}) copy-start(bf16[2,384]{1,0:T(2,128)(2,1)} %param.22) | copy-start | bytes 4612
  0.7 4.3 %copy-start.10 = (bf16[768]{0:T(1024)(128)(2,1)S(1)}, bf16[768]{0:T(1024)(128)(2,1)}, u32[]{:S(2)}) copy-start(bf16[768]{0:T(1024)(128)(2,1)} %param.19) | copy-start | bytes 4612
  0.7 4.6 %copy-start.11 = (bf16[768]{0:T(1024)(128)(2,1)S(1)}, bf16[768]{0:T(1024)(128)(2,1)}, u32[]{:S(2)}) copy-start(bf16[768]{0:T(1024)(128)(2,1)} %param.20) | copy-start | bytes 4612
  0.7 4.8 %copy-start.12 = (bf16[768]{0:T(1024)(128)(2,1)S(1)}, bf16[768]{0:T(1024)(128)(2,1)}, u32[]{:S(2)}) copy-start(bf16[768]{0:T(1024)(128)(2,1)} %param.24) | copy-start | bytes 4612
  0.7 5.0 %copy-start.13 = (bf16[768]{0:T(1024)(128)(2,1)S(1)}, bf16[768]{0:T(1024)(128)(2,1)}, u32[]{:S(2)}) copy-start(bf16[768]{0:T(1024)(128)(2,1)} %param.25) | copy-start | bytes 4612
  0.7 5.2 %copy-start.14 = (bf16[768]{0:T(1024)(128)(2,1)S(1)}, bf16[768]{0:T(1024)(128)(2,1)}, u32[]{:S(2)}) copy-start(bf16[768]{0:T(1024)(128)(2,1)} %param.26) | copy-start | bytes 4612
  0.7 5.4 %copy-start.15 = (bf16[768]{0:T(1024)(128)(2,1)S(1)}, bf16[768]{0:T(1024)(128)(2,1)}, u32[]{:S(2)}) copy-start(bf16[768]{0:T(1024)(128)(2,1)} %param.30) | copy-start | bytes 4612
  0.7 5.8 %copy-start.9 = (bf16[1536]{0:T(1024)(128)(2,1)S(1)}, bf16[1536]{0:T(1024)(128)(2,1)}, u32[]{:S(2)}) copy-start(bf16[1536]{0:T(1024)(128)(2,1)} %param.28) | copy-start | bytes 9220
  0.7 6.6 %copy-start.8 = (s32[2048]{0:T(1024)S(1)}, s32[2048]{0:T(1024)}, u32[]{:S(2)}) copy-start(s32[2048]{0:T(1024)} %param.17) | copy-start | bytes 24580
  4.3 18.4 %collective-permute-start.1 = (f32[3,768,384]{2,1,0:T(8,128)}, f32[3,768,384]{2,1,0:T(8,128)}, u32[]{:S(2)}, u32[]{:S(2)}) collective-permute-start(f32[3,768,384]{2,1,0:T(8,128)} %convert_bitcast_fusion.w_ref.w3_own_ref), channel_id=1, source_target_pairs={{0,1},{1,0},{2,3},{3,2},{4,5},{5,4},{6,7},{7,6},{8,9},{9,8},{10,11... | collective-permute-start | bytes 10616840 | tf_op jit(solution)/shard_map/ppermute | solution.py:902
  4.9 17.7 %copy-start.1 = (f32[384,768]{1,0:T(8,128)}, f32[384,768]{1,0:T(8,128)S(1)}, u32[]{:S(2)}) copy-start(f32[384,768]{1,0:T(8,128)S(1)} %convert_element_type.22.wo_own_ref) | copy-start | bytes 3538948
  4.9 17.8 %collective-permute-start.2 = (f32[384,768]{1,0:T(8,128)S(1)}, f32[384,768]{1,0:T(8,128)S(1)}, u32[]{:S(2)}, u32[]{:S(2)}) collective-permute-start(f32[384,768]{1,0:T(8,128)S(1)} %convert_element_type.22.wo_own_ref), channel_id=1, source_target_pairs={{0,1},{1,0},{2,3},{3,2},{4,5},{5,4},{6,7},{7,6},{8,9},{9,8},{10,11... | collective-permute-start | bytes 3538952 | tf_op jit(solution)/shard_map/ppermute | solution.py:902
  6.8 1.2 copy-start.6
  6.8 15.8 %collective-permute-start = (f32[9,768]{1,0:T(8,128)S(1)}, f32[9,768]{1,0:T(8,128)S(1)}, u32[]{:S(2)}, u32[]{:S(2)}) collective-permute-start(f32[9,768]{1,0:T(8,128)S(1)} %reshape.51.pack_ref), channel_id=1, source_target_pairs={{0,1},{1,0},{2,3},{3,2},{4,5},{5,4},{6,7},{7,6},{8,9},{9,8},{10,11... | collective-permute-start | bytes 82952 | tf_op jit(solution)/shard_map/ppermute | solution.py:902
  22.6 0.6 copy-start.7
  22.7 13.5 %copy-start.3 = (f32[384,768]{1,0:T(8,128)}, f32[384,768]{1,0:T(8,128)S(1)}, u32[]{:S(2)}) copy-start(f32[384,768]{1,0:T(8,128)S(1)} %collective-permute-done.2.wo_other_ref) | copy-start | bytes 3538948
  268.1 4.9 %copy-start = (f32[2048,768]{1,0:T(8,128)S(1)}, f32[2048,768]{1,0:T(8,128)}, u32[]{:S(2)}) copy-start(f32[2048,768]{1,0:T(8,128)} %get-tuple-element.76) | copy-start | bytes 18874372
  268.1 12.5 %slice-start.2 = ((s8[4718592]{0:T(1024)(128)(4,1)}), s8[4194304]{0:T(1024)(128)(4,1)S(1)}, s32[]{:S(2)}) async-start(s8[4718592]{0:T(1024)(128)(4,1)} %bitcast.6), calls=%async_computation.2 | async-start | bytes 8388608
  273.0 4.5 %copy-start.2 = (f32[3,768,384]{2,1,0:T(8,128)S(1)}, f32[3,768,384]{2,1,0:T(8,128)}, u32[]{:S(2)}) copy-start(f32[3,768,384]{2,1,0:T(8,128)} %get-tuple-element.50) | copy-start | bytes 10616836
  273.0 7.6 %slice-start.3 = ((s8[4718592]{0:T(1024)(128)(4,1)}), s8[524288]{0:T(1024)(128)(4,1)S(1)}, s32[]{:S(2)}) async-start(s8[4718592]{0:T(1024)(128)(4,1)} %bitcast.6), calls=%async_computation.3 | async-start | bytes 1048576
  277.5 2.1 copy-start.4
  279.6 4.2 %slice-start = ((s8[4718592]{0:T(1024)(128)(4,1)}), s8[4194304]{0:T(1024)(128)(4,1)S(1)}, s32[]{:S(2)}) async-start(s8[4718592]{0:T(1024)(128)(4,1)} %bitcast.4), calls=%async_computation | async-start | bytes 8388608
  280.6 3.5 %slice-start.1 = ((s8[4718592]{0:T(1024)(128)(4,1)}), s8[524288]{0:T(1024)(128)(4,1)S(1)}, s32[]{:S(2)}) async-start(s8[4718592]{0:T(1024)(128)(4,1)} %bitcast.4), calls=%async_computation.1 | async-start | bytes 1048576
